TPU v7x, 512 devices: a whole 4x4x16 slice. The times are simulated.
512 devices in a mesh: seq: 64 (over z, x_hi, core), head: 8 (over x_lo, y).
Axes of the slice: x: 4 (x_hi: 2, x_lo: 2; x = x_hi * 2 + x_lo), y: 4, z: 16, core: 2. Of those that a mesh axis runs over, the one named last changes fastest.
Arguments:
- attention: bfloat16 [16, 4096, 1536], P(None, 'seq', 'head'), may hold values from -6 to 6
- encoder_skip: bfloat16 [16, 8192, 1536], P('head', 'seq'), may hold values from -6 to 6
- depth_filter: float32 [3, 1536], replicated, may hold values from -3 to 3
- point_weight: bfloat16 [1536, 1536], P('head'), may hold values from -0.15625 to 0.15625
- crop_offset: int32 [16], P('head'), may hold values from 0 to 128
- target_bins: int32 [16, 128], P('head'), may hold values from 0 to 127
- cotangent: bfloat16 [16, 8192, 1536], P('head', 'seq'), may hold values from -6 to 6
Outputs:
- target_rows: bfloat16 [16, 128, 1536], P('head', 'seq')
- attention_grad: bfloat16 [16, 4096, 1536], P('head', 'seq')
- skip_grad: bfloat16 [16, 8192, 1536], P('head', 'seq')
- filter_grad: float32 [3, 1536], replicated
Inputs may be any that keep to these rules, and one draw needn't show every extreme that they name: The cropped window of sequence b starts at bin crop_offset[b]; bins of it past the end of the sequence are empty. Target j of sequence b reads bin 128 * (j // 2) + target_bins[b, j] of the cropped window.
All inputs are finite; a program needn't handle non-finite values.
Results may differ from a plain program's by a relative error of at most 0.007.
Values may be sent and summed in bfloat16 or wider, within the bound.
A program may use at most 64 MiB of HBM per device.

v0:
```python
import math

import jax
import jax.numpy as jnp
from jax import lax
from jax.sharding import PartitionSpec as P

NTD = 2


def extended(shard, sides, width):
    for axis, dim in sides:
        count, length = (lax.axis_size(axis), shard.shape[dim])
        up = [(i, (i + 1) % count) for i in range(count - 1)]
        down = [(j, i) for i, j in up]
        last = lax.slice_in_dim(shard, length - width, length, axis=dim)
        initial = lax.slice_in_dim(shard, 0, width, axis=dim)
        before = lax.ppermute(last, axis, up)
        after = lax.ppermute(initial, axis, down)
        shard = jnp.concatenate([before, shard, after], axis=dim)
    return shard


def passed_along(shard, axis, by):
    count = lax.axis_size(axis)
    pairs = [(i, i + by) for i in range(count) if 0 <= i + by < count]
    return lax.ppermute(shard, axis, pairs)


def gelu_slope(values):
    return (
        0.5 * (1.0 + lax.erf(values * 0.7071067811865476))
        + values * jnp.exp(-0.5 * values * values) * 0.3989422804014327
    )


def with_rims(field):
    return extended(field, (("seq", 1),), 1)


def one_hot(places, length):
    return (places[:, :, None] == jnp.arange(length, dtype=jnp.int32)[None, None, :]).astype(
        jnp.bfloat16
    )


def shards(
    attention, encoder_skip, depth_filter, point_weight, crop_offset, target_bins, cotangent
):
    slab_input = lax.all_to_all(attention, "head", split_axis=0, concat_axis=2, tiled=True)
    local_seqs = encoder_skip.shape[0]
    slab_rows = encoder_skip.shape[1]
    channels = encoder_skip.shape[2]
    summed = (
        jnp.repeat(slab_input, 2, axis=1).astype(jnp.float32) + encoder_skip.astype(jnp.float32)
    ).astype(jnp.bfloat16)
    padded = with_rims(summed)
    filtered = (
        depth_filter[0] * padded[:, :-2]
        + depth_filter[1] * padded[:, 1:-1]
        + depth_filter[2] * padded[:, 2:]
    )
    activated = jax.nn.gelu(filtered, approximate=False).astype(jnp.bfloat16)
    flat_act = activated.reshape(local_seqs * slab_rows, channels)
    full_weight = lax.all_gather(point_weight, "head", axis=0, tiled=True)
    mixed_rows = jnp.dot(flat_act, full_weight, preferred_element_type=jnp.float32)
    block_out = (
        summed.astype(jnp.float32) + mixed_rows.reshape(local_seqs, slab_rows, channels)
    ).astype(jnp.bfloat16)
    slab_index = lax.axis_index("seq")
    my_places = (
        lax.dynamic_slice_in_dim(target_bins, slab_index * NTD, NTD, 1) + crop_offset[:, None]
    )
    next_block = passed_along(block_out, "seq", -1)
    joined = jnp.concatenate([block_out, next_block], axis=1)
    target_rows = jnp.einsum(
        "sjr,srd->sjd",
        one_hot(my_places, 2 * slab_rows),
        joined,
        preferred_element_type=jnp.float32,
    ).astype(jnp.bfloat16)
    prev_cot = passed_along(cotangent, "seq", 1)
    cot_pair = jnp.concatenate([prev_cot, cotangent], axis=1)

    def crop_back(cot_block, shift_by):
        return lax.dynamic_slice_in_dim(cot_block, slab_rows - shift_by, slab_rows, 0)

    grad_out = jax.vmap(crop_back)(cot_pair, crop_offset)
    flat_grad = grad_out.reshape(local_seqs * slab_rows, channels)
    grad_act = lax.dot_general(
        flat_grad, full_weight, (((1,), (1,)), ((), ())), preferred_element_type=jnp.float32
    )
    grad_conv = (grad_act.reshape(local_seqs, slab_rows, channels) * gelu_slope(filtered)).astype(
        jnp.bfloat16
    )
    grad_padded = with_rims(grad_conv)
    grad_sum = (
        grad_out.astype(jnp.float32)
        + depth_filter[0] * grad_padded[:, 2:]
        + depth_filter[1] * grad_padded[:, 1:-1]
        + depth_filter[2] * grad_padded[:, :-2]
    )
    skip_grad = grad_sum.astype(jnp.bfloat16)
    attention_grad = (
        grad_sum.reshape(local_seqs, slab_rows // 2, 2, channels).sum(axis=2).astype(jnp.bfloat16)
    )
    filter_terms = jnp.stack(
        [
            jnp.einsum(
                "srd,srd->d", grad_conv, padded[:, 0:slab_rows], preferred_element_type=jnp.float32
            ),
            jnp.einsum(
                "srd,srd->d",
                grad_conv,
                padded[:, 1 : slab_rows + 1],
                preferred_element_type=jnp.float32,
            ),
            jnp.einsum(
                "srd,srd->d",
                grad_conv,
                padded[:, 2 : slab_rows + 2],
                preferred_element_type=jnp.float32,
            ),
        ]
    )
    filter_sum = lax.psum(filter_terms, ("seq", "head"))
    row_count = local_seqs * lax.axis_size("head") * slab_rows * lax.axis_size("seq")
    filter_grad = filter_sum * (1.0 / math.sqrt(row_count))
    return (target_rows, attention_grad, skip_grad, filter_grad)


def solution(mesh):
    in_specs = (
        P(None, "seq", "head"),
        P("head", "seq", None),
        P(),
        P("head", None),
        P("head"),
        P("head", None),
        P("head", "seq", None),
    )
    out_specs = (P("head", "seq", None), P("head", "seq", None), P("head", "seq", None), P())
    return jax.shard_map(shards, mesh=mesh, in_specs=in_specs, out_specs=out_specs, check_vma=False)
```

profile of v0, /device:TPU:1, one launch (start us, length us, event | category | flops | bytes accessed | tf_op | source)
XLA Modules:
  0.0 225.0 jit_solution(16963135204489975365)
XLA Ops:
  7.2 0.0 copy-start.6
  7.2 0.0 copy-start.4
  7.2 0.0 copy-start.5
  7.2 0.0 all-gather.2.cloned.1.call-start
  7.2 0.7 all-gather.2.cloned.1.call-update
  7.9 6.0 %all-to-all-start = ((bf16[16,64,192]{2,1,0:T(8,128)(2,1)}), bf16[16,64,192]{2,1,0:T(8,128)(2,1)S(1)}, u32[]{:S(2)}, u32[]{:S(2)}) async-start(bf16[16,64,192]{2,1,0:T(8,128)(2,1)} %param.7), calls=%async_computation | async-start | bytes 1048576 | tf_op jit(solution)/shard_map/all_to_all | solution.py:50
  13.9 5.2 %collective-permute-start.3 = (bf16[2,128,1536]{2,1,0:T(8,128)(2,1)}, bf16[2,128,1536]{2,1,0:T(8,128)(2,1)}, u32[]{:S(2)}, u32[]{:S(2)}) collective-permute-start(bf16[2,128,1536]{2,1,0:T(8,128)(2,1)} %param.13), channel_id=1, source_target_pairs={{0,8},{8,16},{16,24},{24,32},{32,40},{40,48},{48,56},{56,64},{64,7... | collective-permute-start | bytes 2359304 | tf_op jit(solution)/shard_map/ppermute | solution.py:27
  19.1 0.0 copy-done.6
  19.2 0.1 copy.13
  19.2 0.0 copy-done.4
  19.2 0.1 slice_reduce_fusion.2
  19.3 0.0 copy-done.5
  19.3 0.1 dynamic-slice_add_fusion
  19.4 1.6 all-to-all-done
  21.0 0.3 copy.36
  21.3 0.3 reshape.54
  21.7 0.5 broadcast_in_dim.4
  22.2 1.1 convert_element_type.67
  23.3 1.3 add_convert_fusion
  24.6 0.0 copy-start
  24.7 7.6 %collective-permute-start = (bf16[2,1,1536]{2,1,0:T(2,128)(2,1)S(1)}, bf16[2,1,1536]{2,1,0:T(2,128)(2,1)S(1)}, u32[]{:S(2)}, u32[]{:S(2)}) collective-permute-start(bf16[2,1,1536]{2,1,0:T(2,128)(2,1)S(1)} %get-tuple-element.40), channel_id=1, source_target_pairs={{0,8},{8,16},{16,24},{24,32},{32,40},{40,48},{48,56},{56,64},{64,7... | collective-permute-start | bytes 18440 | tf_op jit(solution)/shard_map/ppermute | solution.py:18
  32.3 0.0 copy-start.2
  32.3 3.0 %collective-permute-start.1 = (bf16[2,1,1536]{2,1,0:T(2,128)(2,1)S(1)}, bf16[2,1,1536]{2,1,0:T(2,128)(2,1)S(1)}, u32[]{:S(2)}, u32[]{:S(2)}) collective-permute-start(bf16[2,1,1536]{2,1,0:T(2,128)(2,1)S(1)} %get-tuple-element.41), channel_id=1, source_target_pairs={{8,0},{16,8},{24,16},{32,24},{40,32},{48,40},{56,48},{64,56},{72,6... | collective-permute-start | bytes 18440 | tf_op jit(solution)/shard_map/ppermute | solution.py:19
  35.3 0.0 collective-permute-done.3
  35.4 1.5 pad_maximum_fusion
  36.9 0.0 copy-start.1
  36.9 4.0 %while.1 = (s32[]{:T(128)}, bf16[2,256,1536]{2,1,0:T(8,128)(2,1)S(1)}, s32[2,3]{1,0:T(2,128)S(1)}, bf16[2,128,1536]{2,1,0:T(8,128)(2,1)S(1)}, s32[]{:T(128)}) while((s32[]{:T(128)}, bf16[2,256,1536]{2,1,0:T(8,128)(2,1)S(1)}, s32[2,3]{1,0:T(2,128)S(1)}, bf16[2,128,1536]{2,1,0:T(8,128)(2,1)S(1)}, s32[]{:T(128)}) %tuple.38), condition=%wide.while_cond, body=%wide.while_body.sunk | while | flops 2 | bytes 786557 | solution.py:86
  36.9 0.6 fusion.117
  37.5 1.4 dynamic-slice_dynamic-update-slice_fusion.2
  38.9 0.6 fusion.117
  39.5 1.4 dynamic-slice_dynamic-update-slice_fusion.2
  40.9 0.0 collective-permute-done
  40.9 0.0 collective-permute-done.1
  40.9 39.8 %all-gather.2.cloned.1.call-done = bf16[1536,1536]{1,0:T(8,128)(2,1)} async-done(((bf16[192,1536]{1,0:T(8,128)(2,1)}), bf16[1536,1536]{1,0:T(8,128)(2,1)}) %all-gather.2.cloned.1.call-update) | async-done | bytes 4718608 | tf_op jit(solution)/shard_map/all_gather | solution.py:65
  80.8 8.3 %fusion.10 = bf16[2,128,1536]{2,1,0:T(8,128)(2,1)} fusion(bf16[1536,1536]{1,0:T(8,128)(2,1)} %all-gather.2.cloned.1.call-done, bf16[2,128,1536]{2,1,0:T(8,128)(2,1)S(1)} %copy-done.1, bf16[2,1,1536]{2,1,0:T(2,128)(2,1)S(1)} %collective-permute-done.1, bf16[2,1,1536]{2,1,0:T(2,128)(2,1)S(1)} %collective-permute-done, f32[1536]{0:T(1024)S(1)} %get-tuple-element.24, ...), kind=kOutput, calls=%fused_computation.8 | convolution fusion | flops 1240203264 | bytes 6322176 | tf_op jit(solution)/shard_map/dot_general | solution.py:66
  89.1 2.6 %collective-permute-start.2 = (bf16[2,128,1536]{2,1,0:T(8,128)(2,1)}, bf16[2,128,1536]{2,1,0:T(8,128)(2,1)}, u32[]{:S(2)}, u32[]{:S(2)}) collective-permute-start(bf16[2,128,1536]{2,1,0:T(8,128)(2,1)} %fusion.10), channel_id=1, source_target_pairs={{8,0},{16,8},{24,16},{32,24},{40,32},{48,40},{56,48},{64,56},{72,6... | collective-permute-start | bytes 2359304 | tf_op jit(solution)/shard_map/ppermute | solution.py:27
  91.7 2.9 %fusion.25 = (f32[1536]{0:T(1024)S(1)}, f32[1536]{0:T(1024)S(1)}, f32[1536]{0:T(1024)S(1)}, bf16[2,128,1536]{2,1,0:T(8,128)(2,1)S(1)}) fusion(bf16[2,128,1536]{2,1,0:T(8,128)(2,1)S(1)} %copy-done.1, bf16[2,1,1536]{2,1,0:T(2,128)(2,1)S(1)} %collective-permute-done, bf16[2,1,1536]{2,1,0:T(2,128)(2,1)S(1)} %collective-permute-done.1, ...), kind=kOutput, calls=%fused_computation.26 | convolution fusion | flops 1222110720 | bytes 7127040 | tf_op jit(solution)/shard_map/dot_general | solution.py:90
  94.6 106.8 %psum.7 = f32[3,1536]{1,0:T(4,128)S(1)} all-reduce(f32[3,1536]{1,0:T(4,128)S(1)} %pad_maximum_fusion.6), channel_id=1, replica_groups=mesh['seq'=64,'head'=8] {'seq','head'}, use_global_device_ids=true, to_apply=%region_1.0 | all-reduce | flops 4608 | bytes 36864 | tf_op jit(solution)/shard_map/psum | solution.py:126
  201.5 2.9 %collective-permute-start.4 = (bf16[2,1,1536]{2,1,0:T(2,128)(2,1)S(1)}, bf16[2,1,1536]{2,1,0:T(2,128)(2,1)S(1)}, u32[]{:S(2)}, u32[]{:S(2)}) collective-permute-start(bf16[2,1,1536]{2,1,0:T(2,128)(2,1)S(1)} %get-tuple-element.38), channel_id=1, source_target_pairs={{8,0},{16,8},{24,16},{32,24},{40,32},{48,40},{56,48},{64,56},{72,6... | collective-permute-start | bytes 18440 | tf_op jit(solution)/shard_map/ppermute | solution.py:19
  204.4 4.4 %collective-permute-start.5 = (bf16[2,1,1536]{2,1,0:T(2,128)(2,1)S(1)}, bf16[2,1,1536]{2,1,0:T(2,128)(2,1)S(1)}, u32[]{:S(2)}, u32[]{:S(2)}) collective-permute-start(bf16[2,1,1536]{2,1,0:T(2,128)(2,1)S(1)} %get-tuple-element.39), channel_id=1, source_target_pairs={{0,8},{8,16},{16,24},{24,32},{32,40},{40,48},{48,56},{56,64},{64,7... | collective-permute-start | bytes 18440 | tf_op jit(solution)/shard_map/ppermute | solution.py:18
  208.7 0.6 broadcast_multiply_fusion
  209.4 0.0 collective-permute-done.4
  209.4 0.0 collective-permute-done.5
  209.4 2.7 %fusion.111 = (bf16[2,128,1536]{2,1,0:T(8,128)(2,1)}, f32[2,128,1536]{2,1,0:T(8,128)S(1)}) fusion(bf16[2,128,1536]{2,1,0:T(8,128)(2,1)S(1)} %get-tuple-element.42, bf16[2,1,1536]{2,1,0:T(2,128)(2,1)S(1)} %collective-permute-done.5, f32[1536]{0:T(1024)S(1)} %get-tuple-element.24, f32[1536]{0:T(1024)S(1)} %get-tuple-element.25, ...), kind=kLoop, calls=%fused_computation.134 | loop fusion | flops 6684672 | bytes 3962880 | tf_op jit(solution)/shard_map/convert_element_type | solution.py:103
  212.1 0.9 reshape.30
  213.0 2.8 %reduce_sum.9 = bf16[2,64,1536]{2,1,0:T(8,128)(2,1)} reduce(f32[2,64,2,1536]{3,2,1,0:T(2,128)S(1)} %reshape.30, f32[]{:T(128)} %constant.14.clone.1), dimensions={2}, to_apply=%region_0.0 | reduce | flops 196608 | bytes 1966084 | tf_op jit(solution)/shard_map/reduce_sum | solution.py:105
  215.8 0.0 collective-permute-done.2
  215.8 2.3 %convolution_convert_fusion = bf16[2,2,1536]{2,1,0:T(2,128)(2,1)} fusion(bf16[2,128,1536]{2,1,0:T(8,128)(2,1)} %collective-permute-done.2, bf16[2,128,1536]{2,1,0:T(8,128)(2,1)} %fusion.10, s32[2,2]{1,0:T(2,128)S(1)} %dynamic-slice_add_fusion), kind=kOutput, calls=%fused_computation.15 | convolution fusion | flops 6298624 | bytes 1585168 | tf_op jit(solution)/shard_map/sjr,srd->sjd/dot_general | solution.py:76
  (19 shorter events, 0.1 us)
Async XLA Ops:
  7.2 11.9 %copy-start.6 = (s32[2]{0:T(128)S(1)}, s32[2]{0:T(128)}, u32[]{:S(2)}) copy-start(s32[2]{0:T(128)} %param.11) | copy-start | bytes 28
  7.2 12.1 %copy-start.4 = (f32[3,1536]{1,0:T(4,128)S(1)}, f32[3,1536]{1,0:T(4,128)}, u32[]{:S(2)}) copy-start(f32[3,1536]{1,0:T(4,128)} %param.9) | copy-start | bytes 55300
  7.2 12.1 %copy-start.5 = (s32[2,128]{1,0:T(2,128)S(1)}, s32[2,128]{1,0:T(2,128)}, u32[]{:S(2)}) copy-start(s32[2,128]{1,0:T(2,128)} %param.12) | copy-start | bytes 3076
  7.2 73.6 %all-gather.2.cloned.1.call-start = ((), (), s32[]{:S(2)}) async-start(), calls=%async_computation.1 | async-start | bytes 5308416 | tf_op jit(solution)/shard_map/all_gather | solution.py:65
  7.9 13.1 %all-to-all-start = ((bf16[16,64,192]{2,1,0:T(8,128)(2,1)}), bf16[16,64,192]{2,1,0:T(8,128)(2,1)S(1)}, u32[]{:S(2)}, u32[]{:S(2)}) async-start(bf16[16,64,192]{2,1,0:T(8,128)(2,1)} %param.7), calls=%async_computation | async-start | bytes 1048576 | tf_op jit(solution)/shard_map/all_to_all | solution.py:50
  13.9 21.5 %collective-permute-start.3 = (bf16[2,128,1536]{2,1,0:T(8,128)(2,1)}, bf16[2,128,1536]{2,1,0:T(8,128)(2,1)}, u32[]{:S(2)}, u32[]{:S(2)}) collective-permute-start(bf16[2,128,1536]{2,1,0:T(8,128)(2,1)} %param.13), channel_id=1, source_target_pairs={{0,8},{8,16},{16,24},{24,32},{32,40},{40,48},{48,56},{56,64},{64,7... | collective-permute-start | bytes 2359304 | tf_op jit(solution)/shard_map/ppermute | solution.py:27
  24.6 10.7 %copy-start = (bf16[2,128,1536]{2,1,0:T(8,128)(2,1)}, bf16[2,128,1536]{2,1,0:T(8,128)(2,1)S(1)}, u32[]{:S(2)}) copy-start(bf16[2,128,1536]{2,1,0:T(8,128)(2,1)S(1)} %add_convert_fusion) | copy-start | bytes 2359300
  24.7 16.2 %collective-permute-start = (bf16[2,1,1536]{2,1,0:T(2,128)(2,1)S(1)}, bf16[2,1,1536]{2,1,0:T(2,128)(2,1)S(1)}, u32[]{:S(2)}, u32[]{:S(2)}) collective-permute-start(bf16[2,1,1536]{2,1,0:T(2,128)(2,1)S(1)} %get-tuple-element.40), channel_id=1, source_target_pairs={{0,8},{8,16},{16,24},{24,32},{32,40},{40,48},{48,56},{56,64},{64,7... | collective-permute-start | bytes 18440 | tf_op jit(solution)/shard_map/ppermute | solution.py:18
  32.3 4.5 %copy-start.2 = (bf16[2,128,1536]{2,1,0:T(8,128)(2,1)S(1)}, bf16[2,128,1536]{2,1,0:T(8,128)(2,1)}, u32[]{:S(2)}) copy-start(bf16[2,128,1536]{2,1,0:T(8,128)(2,1)} %custom-call) | copy-start | bytes 2359300
  32.3 8.6 %collective-permute-start.1 = (bf16[2,1,1536]{2,1,0:T(2,128)(2,1)S(1)}, bf16[2,1,1536]{2,1,0:T(2,128)(2,1)S(1)}, u32[]{:S(2)}, u32[]{:S(2)}) collective-permute-start(bf16[2,1,1536]{2,1,0:T(2,128)(2,1)S(1)} %get-tuple-element.41), channel_id=1, source_target_pairs={{8,0},{16,8},{24,16},{32,24},{40,32},{48,40},{56,48},{64,56},{72,6... | collective-permute-start | bytes 18440 | tf_op jit(solution)/shard_map/ppermute | solution.py:19
  36.9 43.9 %copy-start.1 = (bf16[2,128,1536]{2,1,0:T(8,128)(2,1)S(1)}, bf16[2,128,1536]{2,1,0:T(8,128)(2,1)}, u32[]{:S(2)}) copy-start(bf16[2,128,1536]{2,1,0:T(8,128)(2,1)} %copy-done) | copy-start | bytes 2359300
  40.9 50.8 %copy-start.3 = (bf16[2,128,1536]{2,1,0:T(8,128)(2,1)}, bf16[2,128,1536]{2,1,0:T(8,128)(2,1)S(1)}, u32[]{:S(2)}) copy-start(bf16[2,128,1536]{2,1,0:T(8,128)(2,1)S(1)} %get-tuple-element.11) | copy-start | bytes 2359300
  80.8 10.9 %copy-start.7 = (bf16[1536,1536]{1,0:T(8,128)(2,1)S(1)}, bf16[1536,1536]{1,0:T(8,128)(2,1)}, u32[]{:S(2)}) copy-start(bf16[1536,1536]{1,0:T(8,128)(2,1)} %all-gather.2.cloned.1.call-done) | copy-start | bytes 14155780
  89.1 126.7 %collective-permute-start.2 = (bf16[2,128,1536]{2,1,0:T(8,128)(2,1)}, bf16[2,128,1536]{2,1,0:T(8,128)(2,1)}, u32[]{:S(2)}, u32[]{:S(2)}) collective-permute-start(bf16[2,128,1536]{2,1,0:T(8,128)(2,1)} %fusion.10), channel_id=1, source_target_pairs={{8,0},{16,8},{24,16},{32,24},{40,32},{48,40},{56,48},{64,56},{72,6... | collective-permute-start | bytes 2359304 | tf_op jit(solution)/shard_map/ppermute | solution.py:27
  201.5 7.9 %collective-permute-start.4 = (bf16[2,1,1536]{2,1,0:T(2,128)(2,1)S(1)}, bf16[2,1,1536]{2,1,0:T(2,128)(2,1)S(1)}, u32[]{:S(2)}, u32[]{:S(2)}) collective-permute-start(bf16[2,1,1536]{2,1,0:T(2,128)(2,1)S(1)} %get-tuple-element.38), channel_id=1, source_target_pairs={{8,0},{16,8},{24,16},{32,24},{40,32},{48,40},{56,48},{64,56},{72,6... | collective-permute-start | bytes 18440 | tf_op jit(solution)/shard_map/ppermute | solution.py:19
  204.4 5.0 %collective-permute-start.5 = (bf16[2,1,1536]{2,1,0:T(2,128)(2,1)S(1)}, bf16[2,1,1536]{2,1,0:T(2,128)(2,1)S(1)}, u32[]{:S(2)}, u32[]{:S(2)}) collective-permute-start(bf16[2,1,1536]{2,1,0:T(2,128)(2,1)S(1)} %get-tuple-element.39), channel_id=1, source_target_pairs={{0,8},{8,16},{16,24},{24,32},{32,40},{40,48},{48,56},{56,64},{64,7... | collective-permute-start | bytes 18440 | tf_op jit(solution)/shard_map/ppermute | solution.py:18
Sparse Core Ops, SparseCore 0:
  10.1 70.6 all-gather.1
where the time goes:
time: 227 us; the launch traced here: 225 us
  blocking collectives  107 us (47%)
  waiting for transfers between devices  42.2 us (19%)
  starting transfers between devices  31.6 us (14%)
  between operations  14.3 us (6%)
  matrix products  13.5 us (6%)
  other arithmetic  9.01 us (4%)
  local copies, waits for them, and re-layouts  7.43 us (3%)
    psum x1, blocking collectives, shards(): filter_sum = lax.psum(filter_terms, ('seq', 'head'))  107 us
    all_gather x1, waiting for transfers between devices, shards(): full_weight = lax.all_gather(point_weight, 'head', axis=0, tiled=True)  39.8 us
    ppermute x2, starting transfers between devices, extended(): before = lax.ppermute(last, axis, up)  12 us
    dot_general x1, matrix products, shards(): jnp.dot(flat_act, full_weight, preferred_element_type=jnp.float32)  8.3 us
    ppermute x2, starting transfers between devices, passed_along(): return lax.ppermute(shard, axis, pairs)  7.76 us
    all_to_all x1, starting transfers between devices, shards(): lax.all_to_all(attention, 'head', split_axis=0, concat_axis=2, tiled=True)  5.96 us
    ppermute x2, starting transfers between devices, extended(): after = lax.ppermute(initial, axis, down)  5.86 us
  transfers between devices with their start and end apart: 8, of which 2 were waited for; matrix products, arithmetic and copies ran while one was open for 9% of the time, Pallas kernels for 0%

commit v1 on v0

v1 whole, which is shorter than its diff:
```python
import math

import jax
import jax.numpy as jnp
from jax import lax
from jax.experimental import pallas as pl
from jax.experimental.pallas import tpu as pltpu
from jax.sharding import PartitionSpec as P

MESH = pl.DeviceIdType.MESH
ANY = pl.BlockSpec(memory_space=pl.ANY)
VM = pl.BlockSpec(memory_space=pltpu.VMEM)
SM = pl.BlockSpec(memory_space=pltpu.SMEM)
F32 = jnp.float32
BF16 = jnp.bfloat16

D = 1536
HEADS = 8
SEQ = 64
KD = D // HEADS
ROWS = 128
HALF = 64
LOCAL = 2
TILE = 128
OWNERS = D // TILE
PLANE = 32
ZS = 16
PAD = 8
SCALE = 1.0 / math.sqrt(131072.0)


def dot(a, b):
    return jnp.dot(a, b, preferred_element_type=F32)


def dot_t(a, b):
    return lax.dot_general(a, b, (((1,), (1,)), ((), ())), preferred_element_type=F32)


def kernel(
    att,
    skip,
    filt,
    weight,
    offset,
    bins,
    cot,
    tgt_out,
    att_out,
    skip_out,
    filt_out,
    attbuf,
    skipbuf,
    wbuf,
    cotbuf,
    summed,
    slope,
    gout,
    conv,
    edge_s,
    edge_r,
    edge2_s,
    edge2_r,
    rows_s,
    rows_r,
    terms,
    plane_r,
    zsum,
    z_r,
    final,
    fin_r,
    sbf,
    abf,
    pair,
    local_sem,
    att_ss,
    att_rs,
    wy_ss,
    wy_rs,
    wx_ss,
    wx_rs,
    wz_ss,
    wz_rs,
    wc_ss,
    wc_rs,
    cot_sem,
    edge_ss,
    edge_rs,
    edge2_ss,
    edge2_rs,
    rows_sem,
    red_ss,
    red_rs,
):
    s, h = lax.axis_index("seq"), lax.axis_index("head")
    z, xh, c = s // 4, (s // 2) % 2, s % 2
    xl, y = h // 4, h % 4
    x = 2 * xh + xl
    zp = z % 2

    def at(z_, xh_, c_, xl_, y_):
        return ((z_ * 2 + xh_) * 2 + c_, xl_ * 4 + y_)

    def x_peer(by):
        other = (x + by + 4) % 4
        return at(z, other // 2, c, other % 2, y)

    def y_peer(by):
        return (s, xl * 4 + (y + by + 8) % 4)

    def z_peer(by):
        return at((z + by + 2 * ZS) % ZS, xh, c, xl, y)

    core_peer = at(z, xh, 1 - c, xl, y)
    next_dev = ((s + 1) % SEQ, h)
    prev_dev = ((s + SEQ - 1) % SEQ, h)

    def plane_dev(r):
        return at(z, (r // 8) % 2, r // 16, (r // 4) % 2, r % 4)

    my_plane = c * 16 + xh * 8 + xl * 4 + y

    def owner(t):
        return t + 16 * (t % 2)

    own_w = pltpu.make_async_copy(weight, wbuf.at[pl.ds(h * KD, KD)], local_sem.at[0])
    own_skip = pltpu.make_async_copy(skip, skipbuf, local_sem.at[1])
    own_cot = pltpu.make_async_copy(cot, cotbuf.at[:, pl.ds(ROWS, ROWS)], local_sem.at[2])
    own_att = pltpu.make_async_copy(att.at[pl.ds(LOCAL * h, LOCAL)], attbuf.at[h], local_sem.at[3])
    own_w.start()
    own_att.start()
    own_skip.start()
    own_cot.start()

    barrier = pltpu.get_barrier_semaphore()

    @pl.loop(1, PLANE)
    def _(i):
        pl.semaphore_signal(barrier, inc=1, device_id=plane_dev((my_plane + i) % PLANE), device_id_type=MESH)

    @pl.loop(1, ZS)
    def _(i):
        pl.semaphore_signal(barrier, inc=1, device_id=z_peer(i), device_id_type=MESH)

    pl.semaphore_signal(barrier, inc=1, device_id=next_dev, device_id_type=MESH)
    pl.semaphore_signal(barrier, inc=1, device_id=prev_dev, device_id_type=MESH)
    pl.semaphore_wait(barrier, PLANE - 1 + ZS - 1 + 2)

    def remote(src, dst, ss, rs, dev):
        return pltpu.make_async_remote_copy(
            src_ref=src, dst_ref=dst, send_sem=ss, recv_sem=rs, device_id=dev, device_id_type=MESH
        )

    att_copies = []
    for i in range(1, HEADS):
        to = (h + i) % HEADS
        cp = remote(
            att.at[pl.ds(LOCAL * to, LOCAL)], attbuf.at[h], att_ss.at[i - 1], att_rs.at[i - 1], (s, to)
        )
        cp.start()
        att_copies.append(cp)

    QUARTER = KD // 4

    def shard_row(xl_, d):
        return (xl_ * 4 + (y + d) % 4) * KD + c * (KD // 2)

    def piece(row, n):
        return wbuf.at[pl.ds(pl.multiple_of(row, 16), n)]

    own_half = weight.at[pl.ds(pl.multiple_of(c * (KD // 2), 16), KD // 2)]
    wy = []
    for d in (1, 3, 2):
        cp = remote(own_half, piece(h * KD + c * (KD // 2), KD // 2), wy_ss.at[d - 1], wy_rs.at[d - 1], y_peer(-d))
        cp.start()
        wy.append(cp)

    def x_copies(j):
        d = j + zp * (3 - 2 * j)
        row = shard_row(xl, d)
        return [
            remote(
                piece(row + p * QUARTER, QUARTER),
                piece(row + p * QUARTER, QUARTER),
                wx_ss.at[j, p],
                wx_rs.at[j, p],
                x_peer(1 - 2 * p),
            )
            for p in range(2)
        ]

    def x_arrived(j, p):
        d = j + zp * (3 - 2 * j)
        return piece(shard_row(1 - xl, d) + p * QUARTER, QUARTER)

    def z_arrived(j, p):
        d = j + (1 - zp) * (3 - 2 * j)
        return piece(shard_row(1 - xl, d) + p * QUARTER, QUARTER)

    core_copies = []

    def to_core(ref):
        k = len(core_copies)
        cp = remote(ref, ref, wc_ss.at[k], wc_rs.at[k], core_peer)
        cp.start()
        core_copies.append(cp)

    cot_copy = remote(cot, cotbuf.at[:, pl.ds(0, ROWS)], cot_sem.at[0], cot_sem.at[1], next_dev)
    cot_copy.start()

    own_w.wait()
    x0, x1 = x_copies(0), x_copies(1)

    @pl.when(zp == 0)
    def _():
        for cp in x0:
            cp.start()

    own_skip.wait()
    own_att.wait()
    for cp in att_copies:
        cp.wait()
    up = (
        lax.broadcasted_iota(jnp.int32, (ROWS, HALF), 0) // 2
        == lax.broadcasted_iota(jnp.int32, (ROWS, HALF), 1)
    ).astype(BF16)
    for b in range(LOCAL):
        for k in range(HEADS // 2):
            wide = jnp.concatenate([dot(up, attbuf[2 * k, b]), dot(up, attbuf[2 * k + 1, b])], axis=1)
            cols = pl.ds(2 * KD * k, 2 * KD)
            both = (wide + skipbuf[b, :, cols].astype(F32)).astype(BF16)
            sbf[pl.ds(b * ROWS, ROWS), cols] = both
            summed[b, pl.ds(PAD, ROWS), cols] = both.astype(F32)
        edge_s[0, pl.ds(b, 1), :] = summed[b, pl.ds(PAD, 1), :]
        edge_s[1, pl.ds(b, 1), :] = summed[b, pl.ds(PAD + ROWS - 1, 1), :]
    edges = [
        remote(edge_s.at[0], edge_r.at[1], edge_ss.at[0], edge_rs.at[1], prev_dev),
        remote(edge_s.at[1], edge_r.at[0], edge_ss.at[1], edge_rs.at[0], next_dev),
    ]
    for cp in edges:
        cp.start()

    for i, d in enumerate((1, 3, 2)):
        wy[i].wait_recv()
        if d == 1:

            @pl.when(zp == 0)
            def _():
                for cp in x1:
                    cp.start()

        if d == 3:

            @pl.when(zp == 1)
            def _():
                for cp in x0:
                    cp.start()

        if d == 2:

            @pl.when(zp == 1)
            def _():
                for cp in x1:
                    cp.start()

        to_core(piece(shard_row(xl, d), KD // 2))

    for cp in edges:
        cp.wait_recv()
    first, last = (s > 0).astype(F32), (s < SEQ - 1).astype(F32)
    for b in range(LOCAL):
        summed[b, pl.ds(PAD - 1, 1), :] = edge_r[0, pl.ds(b, 1), :] * first
        summed[b, pl.ds(PAD + ROWS, 1), :] = edge_r[1, pl.ds(b, 1), :] * last

    def forward(b):
        @pl.loop(0, D // TILE)
        def _(t):
            cols = pl.ds(pl.multiple_of(t * TILE, TILE), TILE)
            taps = filt[:, cols]
            v = (
                taps[0:1] * summed[b, pl.ds(PAD - 1, ROWS), cols]
                + taps[1:2] * summed[b, pl.ds(PAD, ROWS), cols]
                + taps[2:3] * summed[b, pl.ds(PAD + 1, ROWS), cols]
            )
            phi = 0.5 * (1.0 + lax.erf(v * 0.7071067811865476))
            abf[pl.ds(b * ROWS, ROWS), cols] = (v * phi).astype(BF16)
            slope[b, :, cols] = phi + v * jnp.exp(-0.5 * v * v) * 0.3989422804014327

    z_copies = [[None, None], [None, None]]
    for j in range(2):
        forward(j)
        for p in range(2):
            x0_or_1 = (x0, x1)[j]
            x0_or_1[p].wait_recv()
            ref = x_arrived(j, p)
            cp = remote(ref, ref, wz_ss.at[j, p], wz_rs.at[j, p], z_peer(1 - 2 * p))
            cp.start()
            z_copies[j][p] = cp
            to_core(ref)

    own_cot.wait()
    cot_copy.wait()
    place = lax.broadcasted_iota(jnp.int32, (ROWS, 2 * ROWS), 1)
    row = lax.broadcasted_iota(jnp.int32, (ROWS, 2 * ROWS), 0)
    for b in range(LOCAL):
        chosen = (place == row + (ROWS - offset[b])) & ((place >= ROWS) | (s > 0))
        moved = dot(chosen.astype(BF16), cotbuf[b])
        gout[pl.ds(b * ROWS, ROWS), :] = moved.astype(BF16)

    pick = lax.broadcasted_iota(jnp.int32, (16, LOCAL * ROWS), 0)
    spot = lax.broadcasted_iota(jnp.int32, (16, LOCAL * ROWS), 1)
    hit = jnp.zeros((16, LOCAL * ROWS), jnp.bool_)
    before = jnp.maximum(s - 1, 0)
    for b in range(LOCAL):
        for j in range(2):
            mine = bins[b, 2 * s + j] + offset[b]
            theirs = bins[b, 2 * before + j] + offset[b] - ROWS
            hit = hit | (
                (pick == 2 * b + j) & (spot == mine + b * ROWS) & (spot < (b + 1) * ROWS)
            )
            hit = hit | (
                (pick == 4 + 2 * b + j) & (spot == theirs + b * ROWS) & (spot >= b * ROWS) & (s > 0)
            )
    hit = hit.astype(BF16)
    act_rows = dot(hit, abf[...]).astype(BF16)
    sum_rows = dot(hit, sbf[...])

    for j in range(2):
        for p in range(2):
            z_copies[j][p].wait_recv()
            to_core(z_arrived(j, p))
    for cp in core_copies:
        cp.wait_recv()

    block_rows = (sum_rows + dot(act_rows, wbuf[...])).astype(BF16).astype(F32)
    rows_s[...] = block_rows[0:8]
    rows_copy = remote(rows_s.at[pl.ds(4, 4)], rows_r, rows_sem.at[0], rows_sem.at[1], prev_dev)
    rows_copy.start()

    for t in range(D // 256):
        cols = pl.ds(t * 256, 256)
        ga = dot_t(gout[...], wbuf[cols, :])
        sums = [0.0, 0.0, 0.0]
        for b in range(LOCAL):
            gc = (ga[b * ROWS : (b + 1) * ROWS] * slope[b, :, cols]).astype(BF16).astype(F32)
            conv[b, pl.ds(PAD, ROWS), cols] = gc
            for k in range(3):
                sums[k] = sums[k] + jnp.sum(
                    gc * summed[b, pl.ds(PAD - 1 + k, ROWS), cols], axis=0, keepdims=True
                )
        for k in range(3):
            for u in range(2):
                terms[2 * t + u, pl.ds(k, 1), :] = sums[k][:, u * TILE : (u + 1) * TILE]
    for t in range(OWNERS):
        terms[t, pl.ds(3, 1), :] = jnp.zeros((1, TILE), F32)
    for b in range(LOCAL):
        edge2_s[0, pl.ds(b, 1), :] = conv[b, pl.ds(PAD, 1), :]
        edge2_s[1, pl.ds(b, 1), :] = conv[b, pl.ds(PAD + ROWS - 1, 1), :]

    for t in range(OWNERS):
        @pl.when(my_plane != owner(t))
        def _():
            remote(
                terms.at[t], plane_r.at[my_plane], red_ss.at[0], red_rs.at[0], plane_dev(owner(t))
            ).start()

        @pl.when(my_plane == owner(t))
        def _():
            plane_r[my_plane] = terms[t]

    edges2 = [
        remote(edge2_s.at[0], edge2_r.at[1], edge2_ss.at[0], edge2_rs.at[1], prev_dev),
        remote(edge2_s.at[1], edge2_r.at[0], edge2_ss.at[1], edge2_rs.at[0], next_dev),
    ]
    for cp in edges2:
        cp.start()

    t_mine = my_plane % 16
    owns = (t_mine < OWNERS) & (my_plane // 16 == t_mine % 2)

    @pl.when(owns)
    def _():
        part = plane_r.at[pl.ds(0, PLANE - 1)]
        pltpu.make_async_copy(part, part, red_rs.at[0]).wait()
        total = plane_r[0]
        for i in range(1, PLANE):
            total = total + plane_r[i]
        zsum[...] = total
        z_r[z] = total
        for i in range(1, ZS):
            remote(zsum, z_r.at[z], red_ss.at[1], red_rs.at[1], z_peer(i)).start()

    for cp in edges2:
        cp.wait()
    for b in range(LOCAL):
        conv[b, pl.ds(PAD - 1, 1), :] = edge2_r[0, pl.ds(b, 1), :] * first
        conv[b, pl.ds(PAD + ROWS, 1), :] = edge2_r[1, pl.ds(b, 1), :] * last
    for b in range(LOCAL):

        @pl.loop(0, D // TILE)
        def _(t):
            cols = pl.ds(pl.multiple_of(t * TILE, TILE), TILE)
            taps = filt[:, cols]
            gs = (
                gout[pl.ds(b * ROWS, ROWS), cols].astype(F32)
                + taps[0:1] * conv[b, pl.ds(PAD + 1, ROWS), cols]
                + taps[1:2] * conv[b, pl.ds(PAD, ROWS), cols]
                + taps[2:3] * conv[b, pl.ds(PAD - 1, ROWS), cols]
            )
            skip_out[b, :, cols] = gs.astype(BF16)
            pair[...] = gs
            att_out[b, :, cols] = (
                pair[pl.ds(0, HALF, stride=2), :] + pair[pl.ds(1, HALF, stride=2), :]
            ).astype(BF16)

    rows_copy.wait()
    for b in range(LOCAL):
        whole = rows_s[pl.ds(2 * b, 2), :] + rows_r[pl.ds(2 * b, 2), :] * last
        tgt_out[b] = whole.astype(BF16)

    @pl.when(owns)
    def _():
        part = z_r.at[pl.ds(0, ZS - 1)]
        pltpu.make_async_copy(part, part, red_rs.at[1]).wait()
        total = z_r[0]
        for i in range(1, ZS):
            total = total + z_r[i]
        final[...] = total * SCALE
        fin_r[t_mine] = total * SCALE

        @pl.loop(1, PLANE)
        def _(i):
            remote(
                final, fin_r.at[t_mine], red_ss.at[2], red_rs.at[2], plane_dev((my_plane + i) % PLANE)
            ).start()

    @pl.when(owns)
    def _():
        part = fin_r.at[pl.ds(0, OWNERS - 1)]
        pltpu.make_async_copy(part, part, red_rs.at[2]).wait()

    @pl.when(jnp.logical_not(owns))
    def _():
        pltpu.make_async_copy(fin_r, fin_r, red_rs.at[2]).wait()

    for t in range(OWNERS):
        filt_out[:, pl.ds(t * TILE, TILE)] = fin_r[t, pl.ds(0, 3), :]

    for i in range(3):
        wy[i].wait_send()
    for cp in x0 + x1 + z_copies[0] + z_copies[1] + core_copies + edges:
        cp.wait_send()

    @pl.when(owns)
    def _():
        part = plane_r.at[pl.ds(0, OWNERS - 1)]
        pltpu.make_async_copy(part, part, red_ss.at[0]).wait()
        part = z_r.at[pl.ds(0, ZS - 1)]
        pltpu.make_async_copy(part, part, red_ss.at[1]).wait()
        part = plane_r.at[pl.ds(0, PLANE - 1)]
        pltpu.make_async_copy(part, part, red_ss.at[2]).wait()

    @pl.when(jnp.logical_not(owns))
    def _():
        part = plane_r.at[pl.ds(0, OWNERS)]
        pltpu.make_async_copy(part, part, red_ss.at[0]).wait()


def shards(attention, encoder_skip, depth_filter, point_weight, crop_offset, target_bins, cotangent):
    dma = pltpu.SemaphoreType.DMA
    wide = ROWS + 2 * PAD
    return pl.pallas_call(
        kernel,
        out_shape=(
            jax.ShapeDtypeStruct((LOCAL, 2, D), BF16),
            jax.ShapeDtypeStruct((LOCAL, HALF, D), BF16),
            jax.ShapeDtypeStruct((LOCAL, ROWS, D), BF16),
            jax.ShapeDtypeStruct((3, D), F32),
        ),
        in_specs=[ANY, ANY, VM, ANY, SM, SM, ANY],
        out_specs=(VM, VM, VM, VM),
        scratch_shapes=[
            pltpu.VMEM((HEADS, LOCAL, HALF, KD), BF16),
            pltpu.VMEM((LOCAL, ROWS, D), BF16),
            pltpu.VMEM((D, D), BF16),
            pltpu.VMEM((LOCAL, 2 * ROWS, D), BF16),
            pltpu.VMEM((LOCAL, wide, D), F32),
            pltpu.VMEM((LOCAL, ROWS, D), F32),
            pltpu.VMEM((LOCAL * ROWS, D), BF16),
            pltpu.VMEM((LOCAL, wide, D), F32),
            pltpu.VMEM((2, LOCAL, D), F32),
            pltpu.VMEM((2, LOCAL, D), F32),
            pltpu.VMEM((2, LOCAL, D), F32),
            pltpu.VMEM((2, LOCAL, D), F32),
            pltpu.VMEM((8, D), F32),
            pltpu.VMEM((4, D), F32),
            pltpu.VMEM((OWNERS, 4, TILE), F32),
            pltpu.VMEM((PLANE, 4, TILE), F32),
            pltpu.VMEM((4, TILE), F32),
            pltpu.VMEM((ZS, 4, TILE), F32),
            pltpu.VMEM((4, TILE), F32),
            pltpu.VMEM((OWNERS, 4, TILE), F32),
            pltpu.VMEM((LOCAL * ROWS, D), BF16),
            pltpu.VMEM((LOCAL * ROWS, D), BF16),
            pltpu.VMEM((ROWS, TILE), F32),
            dma((4,)),
            dma((HEADS - 1,)),
            dma((HEADS - 1,)),
            dma((3,)),
            dma((3,)),
            dma((2, 2)),
            dma((2, 2)),
            dma((2, 2)),
            dma((2, 2)),
            dma((11,)),
            dma((11,)),
            dma((2,)),
            dma((2,)),
            dma((2,)),
            dma((2,)),
            dma((2,)),
            dma((2,)),
            dma((3,)),
            dma((3,)),
        ],
        compiler_params=pltpu.CompilerParams(
            collective_id=0, has_side_effects=True, vmem_limit_bytes=48 << 20
        ),
    )(attention, encoder_skip, depth_filter, point_weight, crop_offset, target_bins, cotangent)


def solution(mesh):
    in_specs = (
        P(None, "seq", "head"),
        P("head", "seq", None),
        P(),
        P("head", None),
        P("head"),
        P("head", None),
        P("head", "seq", None),
    )
    out_specs = (P("head", "seq", None), P("head", "seq", None), P("head", "seq", None), P())
    return jax.shard_map(shards, mesh=mesh, in_specs=in_specs, out_specs=out_specs, check_vma=False)
```

time: 227 us -> 81.4 us (0.36)
  blocking collectives: 107 us -> 0 us
  Pallas kernels: 0 us -> 71.1 us
  waiting for transfers between devices: 42.2 us -> 0 us
  starting transfers between devices: 31.6 us -> 0 us
  between operations: 14.3 us -> 0.66 us
  matrix products: 13.5 us -> 0 us
  other arithmetic: 9.01 us -> 0 us
    psum x1 -> x0, blocking collectives: 107 us -> none  [shards(): filter_sum = lax.psum(filter_terms, ('seq', 'head'))]
    pallas_call x0 -> x1, Pallas kernels: none -> 71.1 us  [shards(): pl.pallas_call(kernel, out_shape=(jax.ShapeDtypeStruct((LOCAL, 2, D), BF1...]
    all_gather x1 -> x0, waiting for transfers between devices: 39.8 us -> none  [shards(): full_weight = lax.all_gather(point_weight, 'head', axis=0, tiled=True)]
    ppermute x6 -> x0, starting transfers between devices: 25.6 us -> none  [the longest x2 12 us: extended(): before = lax.ppermute(last, axis, up)]
    dot_general x3 -> x0, matrix products: 13.5 us -> none  [the longest x1 8.3 us: shards(): jnp.dot(flat_act, full_weight, preferred_element_type=jnp.float32)]
    unnamed x18, local copies, waits for them, and re-layouts: 0.13 us -> 9.27 us
    all_to_all x1 -> x0, starting transfers between devices: 5.96 us -> none  [shards(): lax.all_to_all(attention, 'head', split_axis=0, concat_axis=2, tiled=True)]
    convert_element_type x2 -> x0, other arithmetic: 3.99 us -> none  [the longest x1 2.68 us: shards(): skip_grad = grad_sum.astype(jnp.bfloat16)]
  transfers between devices with their start and end apart: 8 -> 0, of which waited for: 2 -> 0; matrix products, arithmetic and copies ran while one was open for 9% -> 0% of each run, Pallas kernels for 0% -> 0%
where the time goes in v1:
time: 81.4 us; the launch traced here: 81 us
  Pallas kernels  71.1 us (87%)
  local copies, waits for them, and re-layouts  9.27 us (11%)
    pallas_call x1, Pallas kernels, shards(): pl.pallas_call(kernel, out_shape=(jax.ShapeDtypeStruct((LOCAL, 2, D), BF1...  71.1 us
    unnamed x18, local copies, waits for them, and re-layouts  9.27 us

profile of v1, /device:TPU:1, one launch (start us, length us, event | category | flops | bytes accessed | tf_op | source)
XLA Modules:
  0.0 81.0 jit_solution(3361071337668194582)
XLA Ops:
  0.6 0.0 copy-start
  0.6 1.1 %copy-done = bf16[2,128,1536]{2,1,0:T(8,128)(2,1)S(1)} copy-done((bf16[2,128,1536]{2,1,0:T(8,128)(2,1)S(1)}, bf16[2,128,1536]{2,1,0:T(8,128)(2,1)}, u32[]{:S(2)}) %copy-start) | copy-done | bytes 786456
  1.8 0.0 copy-start.1
  1.8 1.1 %copy-done.1 = bf16[2,128,1536]{2,1,0:T(8,128)(2,1)S(1)} copy-done((bf16[2,128,1536]{2,1,0:T(8,128)(2,1)S(1)}, bf16[2,128,1536]{2,1,0:T(8,128)(2,1)}, u32[]{:S(2)}) %copy-start.1) | copy-done | bytes 786456
  2.9 0.0 copy-start.2
  2.9 1.1 %copy-done.2 = bf16[192,1536]{1,0:T(8,128)(2,1)S(1)} copy-done((bf16[192,1536]{1,0:T(8,128)(2,1)S(1)}, bf16[192,1536]{1,0:T(8,128)(2,1)}, u32[]{:S(2)}) %copy-start.2) | copy-done | bytes 589848
  4.0 0.0 copy-start.3
  4.0 1.0 %copy-done.3 = bf16[16,64,192]{2,1,0:T(8,128)(2,1)S(1)} copy-done((bf16[16,64,192]{2,1,0:T(8,128)(2,1)S(1)}, bf16[16,64,192]{2,1,0:T(8,128)(2,1)}, u32[]{:S(2)}) %copy-start.3) | copy-done | bytes 393240
  5.0 0.0 copy-start.4
  5.0 0.7 copy-done.4
  5.7 0.0 copy-start.5
  5.7 0.7 copy-done.5
  6.4 0.0 copy-start.6
  6.4 0.7 copy-done.6
  7.1 71.1 %shard_map.102 = (bf16[2,2,1536]{2,1,0:T(2,128)(2,1)S(1)}, bf16[2,64,1536]{2,1,0:T(8,128)(2,1)S(1)}, bf16[2,128,1536]{2,1,0:T(8,128)(2,1)S(1)}, f32[3,1536]{1,0:T(4,128)S(1)}) custom-call(bf16[16,64,192]{2,1,0:T(8,128)(2,1)S(1)} %copy-done.3, bf16[2,128,1536]{2,1,0:T(8,128)(2,1)S(1)} %copy-done, f32[3,1536]{1,0:T(4,128)S(1)} %copy-done.4, ...), custom_call_target="tpu_custom_call" | custom-call | tf_op jit(solution)/shard_map/pallas_call | solution.py:472
  78.2 0.6 copy.15
  78.8 0.7 copy.16
  79.5 0.9 %copy.17 = bf16[2,128,1536]{2,1,0:T(8,128)(2,1)} copy(bf16[2,128,1536]{2,1,0:T(8,128)(2,1)S(1)} %get-tuple-element.10) | data formatting | bytes 1572864
  80.4 0.6 copy.18
Async XLA Ops:
  0.6 1.1 %copy-start = (bf16[2,128,1536]{2,1,0:T(8,128)(2,1)S(1)}, bf16[2,128,1536]{2,1,0:T(8,128)(2,1)}, u32[]{:S(2)}) copy-start(bf16[2,128,1536]{2,1,0:T(8,128)(2,1)} %skip.1) | copy-start | bytes 2359300
  1.8 1.1 %copy-start.1 = (bf16[2,128,1536]{2,1,0:T(8,128)(2,1)S(1)}, bf16[2,128,1536]{2,1,0:T(8,128)(2,1)}, u32[]{:S(2)}) copy-start(bf16[2,128,1536]{2,1,0:T(8,128)(2,1)} %cot.1) | copy-start | bytes 2359300
  2.9 1.1 %copy-start.2 = (bf16[192,1536]{1,0:T(8,128)(2,1)S(1)}, bf16[192,1536]{1,0:T(8,128)(2,1)}, u32[]{:S(2)}) copy-start(bf16[192,1536]{1,0:T(8,128)(2,1)} %weight.1) | copy-start | bytes 1769476
  4.0 1.0 %copy-start.3 = (bf16[16,64,192]{2,1,0:T(8,128)(2,1)S(1)}, bf16[16,64,192]{2,1,0:T(8,128)(2,1)}, u32[]{:S(2)}) copy-start(bf16[16,64,192]{2,1,0:T(8,128)(2,1)} %att.1) | copy-start | bytes 1179652
  5.0 0.7 copy-start.4
  5.7 0.7 copy-start.5
  6.4 0.7 copy-start.6

commit v2 on v1

--- a/solution.py
+++ b/solution.py
@@ -8,9 +8,8 @@
 from jax.sharding import PartitionSpec as P
 
 MESH = pl.DeviceIdType.MESH
-ANY = pl.BlockSpec(memory_space=pl.ANY)
+HBM = pl.BlockSpec(memory_space=pltpu.HBM)
 VM = pl.BlockSpec(memory_space=pltpu.VMEM)
-SM = pl.BlockSpec(memory_space=pltpu.SMEM)
 F32 = jnp.float32
 BF16 = jnp.bfloat16
 
@@ -40,15 +39,20 @@
 def kernel(
     att,
     skip,
+    filt_h,
+    weight,
+    offset_h,
+    bins_h,
+    cot,
+    tgt_out,
+    att_h,
+    skip_h,
+    filt_out,
     filt,
-    weight,
     offset,
     bins,
-    cot,
-    tgt_out,
-    att_out,
-    skip_out,
-    filt_out,
+    attv,
+    apack,
     attbuf,
     skipbuf,
     wbuf,
@@ -72,13 +76,15 @@
     sbf,
     abf,
     pair,
+    att_out,
+    skip_out,
     local_sem,
     att_ss,
     att_rs,
+    wx_ss,
+    wx_rs,
     wy_ss,
     wy_rs,
-    wx_ss,
-    wx_rs,
     wz_ss,
     wz_rs,
     wc_ss,
@@ -91,6 +97,8 @@
     rows_sem,
     red_ss,
     red_rs,
+    plane_in,
+    z_in,
 ):
     s, h = lax.axis_index("seq"), lax.axis_index("head")
     z, xh, c = s // 4, (s // 2) % 2, s % 2
@@ -126,25 +134,42 @@
     own_w = pltpu.make_async_copy(weight, wbuf.at[pl.ds(h * KD, KD)], local_sem.at[0])
     own_skip = pltpu.make_async_copy(skip, skipbuf, local_sem.at[1])
     own_cot = pltpu.make_async_copy(cot, cotbuf.at[:, pl.ds(ROWS, ROWS)], local_sem.at[2])
-    own_att = pltpu.make_async_copy(att.at[pl.ds(LOCAL * h, LOCAL)], attbuf.at[h], local_sem.at[3])
+    own_att = pltpu.make_async_copy(att, attv, local_sem.at[3])
+    small = [
+        pltpu.make_async_copy(filt_h, filt, local_sem.at[4]),
+        pltpu.make_async_copy(offset_h, offset, local_sem.at[5]),
+        pltpu.make_async_copy(bins_h, bins, local_sem.at[6]),
+    ]
+    own_att.start()
     own_w.start()
-    own_att.start()
+    for cp in small:
+        cp.start()
     own_skip.start()
     own_cot.start()
 
     barrier = pltpu.get_barrier_semaphore()
 
-    @pl.loop(1, PLANE)
+    @pl.loop(1, HEADS)
     def _(i):
-        pl.semaphore_signal(barrier, inc=1, device_id=plane_dev((my_plane + i) % PLANE), device_id_type=MESH)
-
-    @pl.loop(1, ZS)
-    def _(i):
-        pl.semaphore_signal(barrier, inc=1, device_id=z_peer(i), device_id_type=MESH)
-
-    pl.semaphore_signal(barrier, inc=1, device_id=next_dev, device_id_type=MESH)
-    pl.semaphore_signal(barrier, inc=1, device_id=prev_dev, device_id_type=MESH)
-    pl.semaphore_wait(barrier, PLANE - 1 + ZS - 1 + 2)
+        pl.semaphore_signal(barrier, inc=1, device_id=(s, (h + i) % HEADS), device_id_type=MESH)
+
+    quad = [at(z, 1 - xh, c, xl, y), core_peer, at(z, 1 - xh, 1 - c, xl, y)]
+    near = quad + [x_peer(1), x_peer(-1), z_peer(1), z_peer(-1), next_dev, prev_dev]
+    for dev in near:
+        pl.semaphore_signal(barrier, inc=1, device_id=dev, device_id_type=MESH)
+    own_att.wait()
+    for i in range(HEADS):
+        apack[i] = jnp.concatenate([attv[LOCAL * i], attv[LOCAL * i + 1]], axis=1)
+    attbuf[h] = apack[h]
+    pl.semaphore_wait(barrier, HEADS - 1 + len(near))
+
+    def greet(sem, dev):
+        pl.semaphore_signal(sem, inc=1, device_id=dev, device_id_type=MESH)
+
+    for dev in quad:
+        greet(plane_in, dev)
+    for by in (1, -1):
+        greet(z_in.at[0], z_peer(by))
 
     def remote(src, dst, ss, rs, dev):
         return pltpu.make_async_remote_copy(
@@ -155,49 +180,19 @@
     for i in range(1, HEADS):
         to = (h + i) % HEADS
         cp = remote(
-            att.at[pl.ds(LOCAL * to, LOCAL)], attbuf.at[h], att_ss.at[i - 1], att_rs.at[i - 1], (s, to)
+            apack.at[to], attbuf.at[h], att_ss.at[i - 1], att_rs.at[i - 1], (s, to)
         )
         cp.start()
         att_copies.append(cp)
 
-    QUARTER = KD // 4
-
-    def shard_row(xl_, d):
-        return (xl_ * 4 + (y + d) % 4) * KD + c * (KD // 2)
-
-    def piece(row, n):
-        return wbuf.at[pl.ds(pl.multiple_of(row, 16), n)]
-
-    own_half = weight.at[pl.ds(pl.multiple_of(c * (KD // 2), 16), KD // 2)]
-    wy = []
-    for d in (1, 3, 2):
-        cp = remote(own_half, piece(h * KD + c * (KD // 2), KD // 2), wy_ss.at[d - 1], wy_rs.at[d - 1], y_peer(-d))
-        cp.start()
-        wy.append(cp)
-
-    def x_copies(j):
-        d = j + zp * (3 - 2 * j)
-        row = shard_row(xl, d)
-        return [
-            remote(
-                piece(row + p * QUARTER, QUARTER),
-                piece(row + p * QUARTER, QUARTER),
-                wx_ss.at[j, p],
-                wx_rs.at[j, p],
-                x_peer(1 - 2 * p),
-            )
-            for p in range(2)
-        ]
-
-    def x_arrived(j, p):
-        d = j + zp * (3 - 2 * j)
-        return piece(shard_row(1 - xl, d) + p * QUARTER, QUARTER)
-
-    def z_arrived(j, p):
-        d = j + (1 - zp) * (3 - 2 * j)
-        return piece(shard_row(1 - xl, d) + p * QUARTER, QUARTER)
-
-    core_copies = []
+    quarter = KD // 4
+
+    def piece(xl_, d, p):
+        row = (xl_ * 4 + (y + d) % 4) * KD + c * (KD // 2) + p * quarter
+        return wbuf.at[pl.ds(pl.multiple_of(row, 16), quarter)]
+
+    own = weight.at[pl.ds(pl.multiple_of(c * (KD // 2) + zp * quarter, 16), quarter)]
+    wy, wx, wz, core_copies = {}, {}, [], []
 
     def to_core(ref):
         k = len(core_copies)
@@ -205,28 +200,47 @@
         cp.start()
         core_copies.append(cp)
 
-    cot_copy = remote(cot, cotbuf.at[:, pl.ds(0, ROWS)], cot_sem.at[0], cot_sem.at[1], next_dev)
-    cot_copy.start()
-
-    own_w.wait()
-    x0, x1 = x_copies(0), x_copies(1)
-
-    @pl.when(zp == 0)
-    def _():
-        for cp in x0:
-            cp.start()
-
+    def to_x(d, src, dst):
+        wx[d] = remote(src, dst, wx_ss.at[d], wx_rs.at[d], x_peer(1 - 2 * (d % 2)))
+        wx[d].start()
+
+    def to_z(other, d):
+        k = len(wz)
+        ref = piece(1 - xl if other else xl, d, zp)
+        cp = remote(ref, ref, wz_ss.at[k], wz_rs.at[k], z_peer(1 - 2 * (k % 2)))
+        cp.start()
+        wz.append((cp, other, d))
+
+    for d in (1, 3, 2):
+        wy[d] = remote(own, piece(xl, 0, zp), wy_ss.at[d - 1], wy_rs.at[d - 1], y_peer(-d))
+        wy[d].start()
+    to_x(0, own, piece(xl, 0, zp))
+
+    def from_y(d):
+        wy[d].wait_recv()
+        ref = piece(xl, d, zp)
+        to_x(d, ref, ref)
+        to_z(False, d)
+        to_core(ref)
+
+    def from_x(d):
+        wx[d].wait_recv()
+        to_z(True, d)
+        to_core(piece(1 - xl, d, zp))
+
+    for cp in small:
+        cp.wait()
     own_skip.wait()
-    own_att.wait()
     for cp in att_copies:
-        cp.wait()
+        cp.wait_recv()
     up = (
         lax.broadcasted_iota(jnp.int32, (ROWS, HALF), 0) // 2
         == lax.broadcasted_iota(jnp.int32, (ROWS, HALF), 1)
     ).astype(BF16)
     for b in range(LOCAL):
         for k in range(HEADS // 2):
-            wide = jnp.concatenate([dot(up, attbuf[2 * k, b]), dot(up, attbuf[2 * k + 1, b])], axis=1)
+            lane = slice(b * KD, (b + 1) * KD)
+            wide = jnp.concatenate([dot(up, attbuf[2 * k])[:, lane], dot(up, attbuf[2 * k + 1])[:, lane]], axis=1)
             cols = pl.ds(2 * KD * k, 2 * KD)
             both = (wide + skipbuf[b, :, cols].astype(F32)).astype(BF16)
             sbf[pl.ds(b * ROWS, ROWS), cols] = both
@@ -240,30 +254,15 @@
     for cp in edges:
         cp.start()
 
-    for i, d in enumerate((1, 3, 2)):
-        wy[i].wait_recv()
-        if d == 1:
-
-            @pl.when(zp == 0)
-            def _():
-                for cp in x1:
-                    cp.start()
-
-        if d == 3:
-
-            @pl.when(zp == 1)
-            def _():
-                for cp in x0:
-                    cp.start()
-
-        if d == 2:
-
-            @pl.when(zp == 1)
-            def _():
-                for cp in x1:
-                    cp.start()
-
-        to_core(piece(shard_row(xl, d), KD // 2))
+    pl.semaphore_wait(z_in.at[0], 2)
+    for by in (2, -2):
+        greet(z_in.at[1], z_peer(by))
+    from_y(1)
+    from_y(3)
+    from_x(0)
+    from_y(2)
+    cot_copy = remote(cot, cotbuf.at[:, pl.ds(0, ROWS)], cot_sem.at[0], cot_sem.at[1], next_dev)
+    cot_copy.start()
 
     for cp in edges:
         cp.wait_recv()
@@ -272,8 +271,8 @@
         summed[b, pl.ds(PAD - 1, 1), :] = edge_r[0, pl.ds(b, 1), :] * first
         summed[b, pl.ds(PAD + ROWS, 1), :] = edge_r[1, pl.ds(b, 1), :] * last
 
-    def forward(b):
-        @pl.loop(0, D // TILE)
+    def forward(b, part):
+        @pl.loop(part * D // TILE // 2, (part + 1) * D // TILE // 2)
         def _(t):
             cols = pl.ds(pl.multiple_of(t * TILE, TILE), TILE)
             taps = filt[:, cols]
@@ -286,17 +285,17 @@
             abf[pl.ds(b * ROWS, ROWS), cols] = (v * phi).astype(BF16)
             slope[b, :, cols] = phi + v * jnp.exp(-0.5 * v * v) * 0.3989422804014327
 
-    z_copies = [[None, None], [None, None]]
-    for j in range(2):
-        forward(j)
-        for p in range(2):
-            x0_or_1 = (x0, x1)[j]
-            x0_or_1[p].wait_recv()
-            ref = x_arrived(j, p)
-            cp = remote(ref, ref, wz_ss.at[j, p], wz_rs.at[j, p], z_peer(1 - 2 * p))
-            cp.start()
-            z_copies[j][p] = cp
-            to_core(ref)
+    forward(0, 0)
+    from_x(1)
+    forward(0, 1)
+    from_x(3)
+    forward(1, 0)
+    from_x(2)
+    pl.semaphore_wait(z_in.at[1], 2)
+    for by in (4, -4):
+        greet(z_in.at[2], z_peer(by))
+    forward(1, 1)
+    own_w.wait()
 
     own_cot.wait()
     cot_copy.wait()
@@ -325,10 +324,9 @@
     act_rows = dot(hit, abf[...]).astype(BF16)
     sum_rows = dot(hit, sbf[...])
 
-    for j in range(2):
-        for p in range(2):
-            z_copies[j][p].wait_recv()
-            to_core(z_arrived(j, p))
+    for cp, other, d in wz:
+        cp.wait_recv()
+        to_core(piece(1 - xl if other else xl, d, 1 - zp))
     for cp in core_copies:
         cp.wait_recv()
 
@@ -357,6 +355,8 @@
         edge2_s[0, pl.ds(b, 1), :] = conv[b, pl.ds(PAD, 1), :]
         edge2_s[1, pl.ds(b, 1), :] = conv[b, pl.ds(PAD + ROWS - 1, 1), :]
 
+    pl.semaphore_wait(plane_in, 3)
+    pl.semaphore_wait(z_in.at[2], 2)
     for t in range(OWNERS):
         @pl.when(my_plane != owner(t))
         def _():
@@ -395,6 +395,7 @@
     for b in range(LOCAL):
         conv[b, pl.ds(PAD - 1, 1), :] = edge2_r[0, pl.ds(b, 1), :] * first
         conv[b, pl.ds(PAD + ROWS, 1), :] = edge2_r[1, pl.ds(b, 1), :] * last
+    out_copies = []
     for b in range(LOCAL):
 
         @pl.loop(0, D // TILE)
@@ -413,6 +414,11 @@
                 pair[pl.ds(0, HALF, stride=2), :] + pair[pl.ds(1, HALF, stride=2), :]
             ).astype(BF16)
 
+        for i, (src, dst) in enumerate(((skip_out, skip_h), (att_out, att_h))):
+            cp = pltpu.make_async_copy(src.at[b], dst.at[b], local_sem.at[7 + 2 * b + i])
+            cp.start()
+            out_copies.append(cp)
+
     rows_copy.wait()
     for b in range(LOCAL):
         whole = rows_s[pl.ds(2 * b, 2), :] + rows_r[pl.ds(2 * b, 2), :] * last
@@ -446,9 +452,9 @@
     for t in range(OWNERS):
         filt_out[:, pl.ds(t * TILE, TILE)] = fin_r[t, pl.ds(0, 3), :]
 
-    for i in range(3):
-        wy[i].wait_send()
-    for cp in x0 + x1 + z_copies[0] + z_copies[1] + core_copies + edges:
+    for cp in out_copies:
+        cp.wait()
+    for cp in att_copies + list(wx.values()) + list(wy.values()) + [w[0] for w in wz] + core_copies + edges:
         cp.wait_send()
 
     @pl.when(owns)
@@ -466,10 +472,23 @@
         pltpu.make_async_copy(part, part, red_ss.at[0]).wait()
 
 
+def finish(a, b, c, d, a_out, b_out, c_out, d_out, av, bv, cv, dv, sem_in, sem_out):
+    parts = ((c, cv, c_out), (b, bv, b_out), (d, dv, d_out), (a, av, a_out))
+    ins = [pltpu.make_async_copy(x, v, sem_in.at[i]) for i, (x, v, _) in enumerate(parts)]
+    outs = [pltpu.make_async_copy(v, o, sem_out.at[i]) for i, (_, v, o) in enumerate(parts)]
+    for cp in ins:
+        cp.start()
+    for cp_in, cp_out in zip(ins, outs):
+        cp_in.wait()
+        cp_out.start()
+    for cp in outs:
+        cp.wait()
+
+
 def shards(attention, encoder_skip, depth_filter, point_weight, crop_offset, target_bins, cotangent):
     dma = pltpu.SemaphoreType.DMA
     wide = ROWS + 2 * PAD
-    return pl.pallas_call(
+    outs = pl.pallas_call(
         kernel,
         out_shape=(
             jax.ShapeDtypeStruct((LOCAL, 2, D), BF16),
@@ -477,10 +496,15 @@
             jax.ShapeDtypeStruct((LOCAL, ROWS, D), BF16),
             jax.ShapeDtypeStruct((3, D), F32),
         ),
-        in_specs=[ANY, ANY, VM, ANY, SM, SM, ANY],
-        out_specs=(VM, VM, VM, VM),
+        in_specs=[HBM] * 7,
+        out_specs=(VM, HBM, HBM, VM),
         scratch_shapes=[
-            pltpu.VMEM((HEADS, LOCAL, HALF, KD), BF16),
+            pltpu.VMEM((3, D), F32),
+            pltpu.SMEM((LOCAL,), jnp.int32),
+            pltpu.SMEM((LOCAL, 128), jnp.int32),
+            pltpu.VMEM((LOCAL * HEADS, HALF, KD), BF16),
+            pltpu.VMEM((HEADS, HALF, LOCAL * KD), BF16),
+            pltpu.VMEM((HEADS, HALF, LOCAL * KD), BF16),
             pltpu.VMEM((LOCAL, ROWS, D), BF16),
             pltpu.VMEM((D, D), BF16),
             pltpu.VMEM((LOCAL, 2 * ROWS, D), BF16),
@@ -503,17 +527,19 @@
             pltpu.VMEM((LOCAL * ROWS, D), BF16),
             pltpu.VMEM((LOCAL * ROWS, D), BF16),
             pltpu.VMEM((ROWS, TILE), F32),
-            dma((4,)),
+            pltpu.VMEM((LOCAL, HALF, D), BF16),
+            pltpu.VMEM((LOCAL, ROWS, D), BF16),
+            dma((11,)),
             dma((HEADS - 1,)),
             dma((HEADS - 1,)),
+            dma((4,)),
+            dma((4,)),
             dma((3,)),
             dma((3,)),
-            dma((2, 2)),
-            dma((2, 2)),
-            dma((2, 2)),
-            dma((2, 2)),
-            dma((11,)),
-            dma((11,)),
+            dma((7,)),
+            dma((7,)),
+            dma((14,)),
+            dma((14,)),
             dma((2,)),
             dma((2,)),
             dma((2,)),
@@ -522,11 +548,21 @@
             dma((2,)),
             dma((3,)),
             dma((3,)),
+            pltpu.SemaphoreType.REGULAR,
+            pltpu.SemaphoreType.REGULAR((3,)),
         ],
         compiler_params=pltpu.CompilerParams(
-            collective_id=0, has_side_effects=True, vmem_limit_bytes=48 << 20
+            collective_id=0, has_side_effects=True, vmem_limit_bytes=60 << 20
         ),
     )(attention, encoder_skip, depth_filter, point_weight, crop_offset, target_bins, cotangent)
+    return pl.pallas_call(
+        finish,
+        out_shape=tuple(jax.ShapeDtypeStruct(o.shape, o.dtype) for o in outs),
+        in_specs=[HBM] * 4,
+        out_specs=(HBM,) * 4,
+        scratch_shapes=[pltpu.VMEM(o.shape, o.dtype) for o in outs] + [dma((4,)), dma((4,))],
+        compiler_params=pltpu.CompilerParams(vmem_limit_bytes=60 << 20),
+    )(*outs)
 
 
 def solution(mesh):

time: 81.4 us -> 71.7 us (0.88)
  local copies, waits for them, and re-layouts: 9.27 us -> 0 us
    unnamed x18 -> x0, local copies, waits for them, and re-layouts: 9.27 us -> none
    pallas_call x1, Pallas kernels: 71.1 us -> 68.7 us  [shards(): pl.pallas_call(kernel, out_shape=(jax.ShapeDtypeStruct((LOCAL, 2, D), BF1...]
    pallas_call x0 -> x1, Pallas kernels: none -> 2.21 us  [shards(): pl.pallas_call(finish, out_shape=tuple((jax.ShapeDtypeStruct(o.shape, o.d...]
where the time goes in v2:
time: 71.7 us; the launch traced here: 71.6 us
  Pallas kernels  70.9 us (99%)
    pallas_call x1, Pallas kernels, shards(): pl.pallas_call(kernel, out_shape=(jax.ShapeDtypeStruct((LOCAL, 2, D), BF1...  68.7 us
    pallas_call x1, Pallas kernels, shards(): pl.pallas_call(finish, out_shape=tuple((jax.ShapeDtypeStruct(o.shape, o.d...  2.21 us

profile of v2, /device:TPU:1, one launch (start us, length us, event | category | flops | bytes accessed | tf_op | source)
XLA Modules:
  0.0 71.6 jit_solution(8887959141689858211)
XLA Ops:
  0.6 68.7 %shard_map.102 = (bf16[2,2,1536]{2,1,0:T(2,128)(2,1)}, bf16[2,64,1536]{2,1,0:T(8,128)(2,1)}, bf16[2,128,1536]{2,1,0:T(8,128)(2,1)}, f32[3,1536]{1,0:T(4,128)}) custom-call(bf16[16,64,192]{2,1,0:T(8,128)(2,1)} %att.1, bf16[2,128,1536]{2,1,0:T(8,128)(2,1)} %skip.1, f32[3,1536]{1,0:T(4,128)} %filt_h.1, bf16[192,1536]{1,0:T(8,128)(2,1)} %weight.1, s32[2]{0:T(128)} %offset_h.1, ...), custom_call_target="tpu_custom_call" | custom-call | tf_op jit(solution)/shard_map/pallas_call | solution.py:491
  69.3 2.2 %shard_map.103 = (bf16[2,2,1536]{2,1,0:T(2,128)(2,1)}, bf16[2,64,1536]{2,1,0:T(8,128)(2,1)}, bf16[2,128,1536]{2,1,0:T(8,128)(2,1)}, f32[3,1536]{1,0:T(4,128)}) custom-call(bf16[2,2,1536]{2,1,0:T(2,128)(2,1)} %get-tuple-element.8.a, bf16[2,64,1536]{2,1,0:T(8,128)(2,1)} %get-tuple-element.9.b, bf16[2,128,1536]{2,1,0:T(8,128)(2,1)} %get-tuple-element.10.c, ...), custom_call_target="tpu_custom_call" | custom-call | tf_op jit(solution)/shard_map/pallas_call | solution.py:558

commit v3 on v2

--- a/solution.py
+++ b/solution.py
@@ -25,6 +25,11 @@
 PLANE = 32
 ZS = 16
 PAD = 8
+BYY = False
+ZL = 2
+COT = 0
+ATT = 2
+Z_SIDES = ((1, -1), (-1, 1), (1, -1), (-1, -1), (1, -1), (-1, 1), (1, -1), (-1, -1))
 SCALE = 1.0 / math.sqrt(131072.0)
 
 
@@ -177,60 +182,129 @@
         )
 
     att_copies = []
-    for i in range(1, HEADS):
-        to = (h + i) % HEADS
-        cp = remote(
-            apack.at[to], attbuf.at[h], att_ss.at[i - 1], att_rs.at[i - 1], (s, to)
-        )
+
+    def start_att():
+        for i in range(1, HEADS):
+            to = (h + i) % HEADS
+            cp = remote(
+                apack.at[to], attbuf.at[h], att_ss.at[i - 1], att_rs.at[i - 1], (s, to)
+            )
+            cp.start()
+            att_copies.append(cp)
+
+    cot_copy = remote(cot, cotbuf.at[:, pl.ds(0, ROWS)], cot_sem.at[0], cot_sem.at[1], next_dev)
+
+    quarter = KD // 4
+
+    def piece(xl_, d, p, lo=0, n=KD // 4):
+        row = (xl_ * 4 + (y + d) % 4) * KD + c * (KD // 2) + p * quarter + lo
+        return wbuf.at[pl.ds(pl.multiple_of(row, 16), n)]
+
+    own = weight.at[pl.ds(pl.multiple_of(c * (KD // 2) + zp * quarter, 16), quarter)]
+    wy, wx, wz, core_copies, sent = {}, {}, [], [], []
+
+    def send(src, dst, ss, rs, k, dev):
+        cp = remote(src, dst, ss.at[k], rs.at[k], dev)
         cp.start()
-        att_copies.append(cp)
-
-    quarter = KD // 4
-
-    def piece(xl_, d, p):
-        row = (xl_ * 4 + (y + d) % 4) * KD + c * (KD // 2) + p * quarter
-        return wbuf.at[pl.ds(pl.multiple_of(row, 16), quarter)]
-
-    own = weight.at[pl.ds(pl.multiple_of(c * (KD // 2) + zp * quarter, 16), quarter)]
-    wy, wx, wz, core_copies = {}, {}, [], []
+        sent.append(cp)
+        return cp
 
     def to_core(ref):
         k = len(core_copies)
-        cp = remote(ref, ref, wc_ss.at[k], wc_rs.at[k], core_peer)
-        cp.start()
-        core_copies.append(cp)
-
-    def to_x(d, src, dst):
-        wx[d] = remote(src, dst, wx_ss.at[d], wx_rs.at[d], x_peer(1 - 2 * (d % 2)))
-        wx[d].start()
-
-    def to_z(other, d):
+        core_copies.append(send(ref, ref, wc_ss, wc_rs, k, core_peer))
+
+    WHOLE, BIG, SMALL = (0, KD // 4), (0, 32), (32, 16)
+
+    def to_x(k, side, d, part, src=None):
+        dst = piece(xl, d, zp, *part)
+        wx[k] = (send(dst if src is None else src, dst, wx_ss, wx_rs, k, x_peer(side)), d, part)
+
+    busy = (0, xh, 1 - xh)[ZL]
+    pair_side = 1 - 2 * xl
+
+    def to_z(other, d, part=WHOLE):
         k = len(wz)
-        ref = piece(1 - xl if other else xl, d, zp)
-        cp = remote(ref, ref, wz_ss.at[k], wz_rs.at[k], z_peer(1 - 2 * (k % 2)))
-        cp.start()
-        wz.append((cp, other, d))
-
-    for d in (1, 3, 2):
-        wy[d] = remote(own, piece(xl, 0, zp), wy_ss.at[d - 1], wy_rs.at[d - 1], y_peer(-d))
-        wy[d].start()
-    to_x(0, own, piece(xl, 0, zp))
-
-    def from_y(d):
-        wy[d].wait_recv()
-        ref = piece(xl, d, zp)
-        to_x(d, ref, ref)
+        calm, full = Z_SIDES[k]
+        side = calm + busy * (full - calm)
+        ref = piece(1 - xl if other else xl, d, zp, *part)
+        wz.append((send(ref, ref, wz_ss, wz_rs, k, z_peer(side)), other, d, part))
+
+    def to_y(k, other, d):
+        dst = piece(1 - xl if other else xl, 0, zp)
+        wy[k] = send(dst if other else own, dst, wy_ss, wy_rs, k, y_peer(-d))
+
+    if ATT == 0:
+        start_att()
+    to_x(0, -pair_side, 0, WHOLE, own)
+    to_y(0, False, 1)
+    to_y(1, False, 3)
+    if COT == 0:
+        cot_copy.start()
+    if ATT == 1:
+        start_att()
+    wy[0].wait_send()
+    wy[1].wait_send()
+    to_y(2, False, 2)
+    if ATT == 2:
+        start_att()
+    if COT == 1:
+        cot_copy.start()
+
+    pl.semaphore_wait(z_in.at[0], 2)
+    for by in (2, -2):
+        greet(z_in.at[1], z_peer(by))
+
+    def from_y(k, d):
+        wy[k].wait_recv()
         to_z(False, d)
-        to_core(ref)
-
-    def from_x(d):
-        wx[d].wait_recv()
-        to_z(True, d)
-        to_core(piece(1 - xl, d, zp))
+        to_core(piece(xl, d, zp))
+
+    def from_x(k):
+        cp, d, part = wx[k]
+        cp.wait_recv()
+        to_z(True, d, part)
+        to_core(piece(1 - xl, d, zp, *part))
+
+    def stage1():
+        from_y(0, 1)
+        if not BYY:
+            to_x(1, pair_side, 1, WHOLE)
+        from_y(1, 3)
+        if not BYY:
+            to_x(2, -pair_side, 3, WHOLE)
+        from_x(0)
+        if BYY:
+            to_y(3, True, 1)
+            to_y(4, True, 3)
+        if COT == 2:
+            cot_copy.start()
+
+    def stage2():
+        from_y(2, 2)
+        to_x(3, pair_side if BYY else -pair_side, 2, BIG)
+        to_x(4, -pair_side if BYY else pair_side, 2, SMALL)
+        if COT == 3:
+            cot_copy.start()
+
+    def stage3(i):
+        if BYY:
+            wy[3 + i].wait_recv()
+            to_z(True, 1 + 2 * i)
+            to_core(piece(1 - xl, 1 + 2 * i, zp))
+        else:
+            from_x(1 + i)
+
+    def stage4():
+        from_x(3)
+        from_x(4)
 
     for cp in small:
         cp.wait()
     own_skip.wait()
+    stage1()
+    pl.semaphore_wait(z_in.at[1], 2)
+    for by in (4, -4):
+        greet(z_in.at[2], z_peer(by))
     for cp in att_copies:
         cp.wait_recv()
     up = (
@@ -245,6 +319,8 @@
             both = (wide + skipbuf[b, :, cols].astype(F32)).astype(BF16)
             sbf[pl.ds(b * ROWS, ROWS), cols] = both
             summed[b, pl.ds(PAD, ROWS), cols] = both.astype(F32)
+        summed[b, pl.ds(PAD - 1, 1), :] = jnp.zeros((1, D), F32)
+        summed[b, pl.ds(PAD + ROWS, 1), :] = jnp.zeros((1, D), F32)
         edge_s[0, pl.ds(b, 1), :] = summed[b, pl.ds(PAD, 1), :]
         edge_s[1, pl.ds(b, 1), :] = summed[b, pl.ds(PAD + ROWS - 1, 1), :]
     edges = [
@@ -254,47 +330,37 @@
     for cp in edges:
         cp.start()
 
-    pl.semaphore_wait(z_in.at[0], 2)
-    for by in (2, -2):
-        greet(z_in.at[1], z_peer(by))
-    from_y(1)
-    from_y(3)
-    from_x(0)
-    from_y(2)
-    cot_copy = remote(cot, cotbuf.at[:, pl.ds(0, ROWS)], cot_sem.at[0], cot_sem.at[1], next_dev)
-    cot_copy.start()
-
-    for cp in edges:
-        cp.wait_recv()
-    first, last = (s > 0).astype(F32), (s < SEQ - 1).astype(F32)
-    for b in range(LOCAL):
-        summed[b, pl.ds(PAD - 1, 1), :] = edge_r[0, pl.ds(b, 1), :] * first
-        summed[b, pl.ds(PAD + ROWS, 1), :] = edge_r[1, pl.ds(b, 1), :] * last
-
-    def forward(b, part):
-        @pl.loop(part * D // TILE // 2, (part + 1) * D // TILE // 2)
+    stage2()
+    def forward(b, low, n, part=0, parts=1):
+        @pl.loop(part * D // TILE // parts, (part + 1) * D // TILE // parts)
         def _(t):
             cols = pl.ds(pl.multiple_of(t * TILE, TILE), TILE)
             taps = filt[:, cols]
             v = (
-                taps[0:1] * summed[b, pl.ds(PAD - 1, ROWS), cols]
-                + taps[1:2] * summed[b, pl.ds(PAD, ROWS), cols]
-                + taps[2:3] * summed[b, pl.ds(PAD + 1, ROWS), cols]
+                taps[0:1] * summed[b, pl.ds(PAD - 1 + low, n), cols]
+                + taps[1:2] * summed[b, pl.ds(PAD + low, n), cols]
+                + taps[2:3] * summed[b, pl.ds(PAD + 1 + low, n), cols]
             )
             phi = 0.5 * (1.0 + lax.erf(v * 0.7071067811865476))
-            abf[pl.ds(b * ROWS, ROWS), cols] = (v * phi).astype(BF16)
-            slope[b, :, cols] = phi + v * jnp.exp(-0.5 * v * v) * 0.3989422804014327
-
-    forward(0, 0)
-    from_x(1)
-    forward(0, 1)
-    from_x(3)
-    forward(1, 0)
-    from_x(2)
-    pl.semaphore_wait(z_in.at[1], 2)
-    for by in (4, -4):
-        greet(z_in.at[2], z_peer(by))
-    forward(1, 1)
+            abf[pl.ds(b * ROWS + low, n), cols] = (v * phi).astype(BF16)
+            slope[b, pl.ds(low, n), cols] = phi + v * jnp.exp(-0.5 * v * v) * 0.3989422804014327
+
+    forward(0, 0, ROWS, 0, 2)
+    stage3(0)
+    stage3(1)
+    forward(0, 0, ROWS, 1, 2)
+    stage4()
+    forward(1, 0, ROWS)
+    for cp in edges:
+        cp.wait_recv()
+    first, last = (s > 0).astype(F32), (s < SEQ - 1).astype(F32)
+    for b in range(LOCAL):
+        summed[b, pl.ds(PAD - 1, 1), :] = edge_r[0, pl.ds(b, 1), :] * first
+        summed[b, pl.ds(PAD + ROWS, 1), :] = edge_r[1, pl.ds(b, 1), :] * last
+
+    for b in range(LOCAL):
+        forward(b, 0, 16)
+        forward(b, ROWS - 16, 16)
     own_w.wait()
 
     own_cot.wait()
@@ -324,9 +390,9 @@
     act_rows = dot(hit, abf[...]).astype(BF16)
     sum_rows = dot(hit, sbf[...])
 
-    for cp, other, d in wz:
+    for cp, other, d, part in wz:
         cp.wait_recv()
-        to_core(piece(1 - xl if other else xl, d, 1 - zp))
+        to_core(piece(1 - xl if other else xl, d, 1 - zp, *part))
     for cp in core_copies:
         cp.wait_recv()
 
@@ -454,7 +520,7 @@
 
     for cp in out_copies:
         cp.wait()
-    for cp in att_copies + list(wx.values()) + list(wy.values()) + [w[0] for w in wz] + core_copies + edges:
+    for cp in att_copies + [q for q in sent if q is not wy[0] and q is not wy[1]] + edges:
         cp.wait_send()
 
     @pl.when(owns)
@@ -532,14 +598,14 @@
             dma((11,)),
             dma((HEADS - 1,)),
             dma((HEADS - 1,)),
-            dma((4,)),
-            dma((4,)),
-            dma((3,)),
-            dma((3,)),
-            dma((7,)),
-            dma((7,)),
-            dma((14,)),
-            dma((14,)),
+            dma((5,)),
+            dma((5,)),
+            dma((5,)),
+            dma((5,)),
+            dma((8,)),
+            dma((8,)),
+            dma((16,)),
+            dma((16,)),
             dma((2,)),
             dma((2,)),
             dma((2,)),

time: 71.7 us -> 68.1 us (0.950)
  Pallas kernels: 70.9 us -> 67.3 us
    pallas_call x1, Pallas kernels: 68.7 us -> 65 us  [shards(): pl.pallas_call(kernel, out_shape=(jax.ShapeDtypeStruct((LOCAL, 2, D), BF1...]
where the time goes in v3:
time: 68.1 us; the launch traced here: 67.9 us
  Pallas kernels  67.3 us (99%)
    pallas_call x1, Pallas kernels, shards(): pl.pallas_call(kernel, out_shape=(jax.ShapeDtypeStruct((LOCAL, 2, D), BF1...  65 us
    pallas_call x1, Pallas kernels, shards(): pl.pallas_call(finish, out_shape=tuple((jax.ShapeDtypeStruct(o.shape, o.d...  2.21 us

profile of v3, /device:TPU:1, one launch (start us, length us, event | category | flops | bytes accessed | tf_op | source)
XLA Modules:
  0.0 67.9 jit_solution(5171374594293447899)
XLA Ops:
  0.6 65.0 %shard_map.102 = (bf16[2,2,1536]{2,1,0:T(2,128)(2,1)}, bf16[2,64,1536]{2,1,0:T(8,128)(2,1)}, bf16[2,128,1536]{2,1,0:T(8,128)(2,1)}, f32[3,1536]{1,0:T(4,128)}) custom-call(bf16[16,64,192]{2,1,0:T(8,128)(2,1)} %att.1, bf16[2,128,1536]{2,1,0:T(8,128)(2,1)} %skip.1, f32[3,1536]{1,0:T(4,128)} %filt_h.1, bf16[192,1536]{1,0:T(8,128)(2,1)} %weight.1, s32[2]{0:T(128)} %offset_h.1, ...), custom_call_target="tpu_custom_call" | custom-call | tf_op jit(solution)/shard_map/pallas_call | solution.py:557
  65.7 2.2 %shard_map.103 = (bf16[2,2,1536]{2,1,0:T(2,128)(2,1)}, bf16[2,64,1536]{2,1,0:T(8,128)(2,1)}, bf16[2,128,1536]{2,1,0:T(8,128)(2,1)}, f32[3,1536]{1,0:T(4,128)}) custom-call(bf16[2,2,1536]{2,1,0:T(2,128)(2,1)} %get-tuple-element.8.a, bf16[2,64,1536]{2,1,0:T(8,128)(2,1)} %get-tuple-element.9.b, bf16[2,128,1536]{2,1,0:T(8,128)(2,1)} %get-tuple-element.10.c, ...), custom_call_target="tpu_custom_call" | custom-call | tf_op jit(solution)/shard_map/pallas_call | solution.py:624

commit v4 on v3

--- a/solution.py
+++ b/solution.py
@@ -390,19 +390,12 @@
     act_rows = dot(hit, abf[...]).astype(BF16)
     sum_rows = dot(hit, sbf[...])
 
-    for cp, other, d, part in wz:
-        cp.wait_recv()
-        to_core(piece(1 - xl if other else xl, d, 1 - zp, *part))
-    for cp in core_copies:
-        cp.wait_recv()
-
-    block_rows = (sum_rows + dot(act_rows, wbuf[...])).astype(BF16).astype(F32)
-    rows_s[...] = block_rows[0:8]
-    rows_copy = remote(rows_s.at[pl.ds(4, 4)], rows_r, rows_sem.at[0], rows_sem.at[1], prev_dev)
-    rows_copy.start()
-
-    for t in range(D // 256):
-        cols = pl.ds(t * 256, 256)
+    pl.semaphore_wait(plane_in, 3)
+    pl.semaphore_wait(z_in.at[2], 2)
+
+    def block(pair_at):
+        start = pl.multiple_of(pair_at * 2 * KD, TILE)
+        cols = pl.ds(start, 2 * KD)
         ga = dot_t(gout[...], wbuf[cols, :])
         sums = [0.0, 0.0, 0.0]
         for b in range(LOCAL):
@@ -412,27 +405,46 @@
                 sums[k] = sums[k] + jnp.sum(
                     gc * summed[b, pl.ds(PAD - 1 + k, ROWS), cols], axis=0, keepdims=True
                 )
-        for k in range(3):
-            for u in range(2):
-                terms[2 * t + u, pl.ds(k, 1), :] = sums[k][:, u * TILE : (u + 1) * TILE]
-    for t in range(OWNERS):
-        terms[t, pl.ds(3, 1), :] = jnp.zeros((1, TILE), F32)
+        for u in range(3):
+            t = 3 * pair_at + u
+            for k in range(3):
+                terms[t, pl.ds(k, 1), :] = sums[k][:, u * TILE : (u + 1) * TILE]
+            terms[t, pl.ds(3, 1), :] = jnp.zeros((1, TILE), F32)
+            to = owner(t)
+
+            @pl.when(my_plane != to)
+            def _():
+                remote(terms.at[t], plane_r.at[my_plane], red_ss.at[0], red_rs.at[0], plane_dev(to)).start()
+
+            @pl.when(my_plane == to)
+            def _():
+                plane_r[my_plane] = terms[t]
+
+    def from_z(*which):
+        for k in which:
+            cp, other, d, part = wz[k]
+            cp.wait_recv()
+            to_core(piece(1 - xl if other else xl, d, 1 - zp, *part))
+
+    def from_core(*which):
+        for k in which:
+            core_copies[k].wait_recv()
+
+    yh = y // 2
+    from_z(0, 1, 2, 3)
+    from_core(0, 1, 8, 9)
+    block(2 * xl + yh)
+    from_z(4, 5)
+    from_core(3, 11)
+    block(2 * xl + 1 - yh)
+    from_z(6, 7)
+    from_core(2, 4, 5, 10, 12, 13)
+    block(2 * (1 - xl) + yh)
+    from_core(6, 7, 14, 15)
+    block(2 * (1 - xl) + 1 - yh)
     for b in range(LOCAL):
         edge2_s[0, pl.ds(b, 1), :] = conv[b, pl.ds(PAD, 1), :]
         edge2_s[1, pl.ds(b, 1), :] = conv[b, pl.ds(PAD + ROWS - 1, 1), :]
-
-    pl.semaphore_wait(plane_in, 3)
-    pl.semaphore_wait(z_in.at[2], 2)
-    for t in range(OWNERS):
-        @pl.when(my_plane != owner(t))
-        def _():
-            remote(
-                terms.at[t], plane_r.at[my_plane], red_ss.at[0], red_rs.at[0], plane_dev(owner(t))
-            ).start()
-
-        @pl.when(my_plane == owner(t))
-        def _():
-            plane_r[my_plane] = terms[t]
 
     edges2 = [
         remote(edge2_s.at[0], edge2_r.at[1], edge2_ss.at[0], edge2_rs.at[1], prev_dev),
@@ -440,6 +452,10 @@
     ]
     for cp in edges2:
         cp.start()
+
+    block_rows = (sum_rows + dot(act_rows, wbuf[...])).astype(BF16).astype(F32)
+    rows_s[...] = block_rows[0:8]
+    rows_copy = remote(rows_s.at[pl.ds(4, 4)], rows_r, rows_sem.at[0], rows_sem.at[1], prev_dev)
 
     t_mine = my_plane % 16
     owns = (t_mine < OWNERS) & (my_plane // 16 == t_mine % 2)
@@ -455,6 +471,8 @@
         z_r[z] = total
         for i in range(1, ZS):
             remote(zsum, z_r.at[z], red_ss.at[1], red_rs.at[1], z_peer(i)).start()
+
+    rows_copy.start()
 
     for cp in edges2:
         cp.wait()
@@ -500,8 +518,7 @@
         final[...] = total * SCALE
         fin_r[t_mine] = total * SCALE
 
-        @pl.loop(1, PLANE)
-        def _(i):
+        for i in range(1, PLANE):
             remote(
                 final, fin_r.at[t_mine], red_ss.at[2], red_rs.at[2], plane_dev((my_plane + i) % PLANE)
             ).start()

time: 68.1 us -> 65.8 us (0.966)
  Pallas kernels: 67.3 us -> 65 us
    pallas_call x1, Pallas kernels: 65 us -> 62.8 us  [shards(): pl.pallas_call(kernel, out_shape=(jax.ShapeDtypeStruct((LOCAL, 2, D), BF1...]
where the time goes in v4:
time: 65.8 us; the launch traced here: 65.6 us
  Pallas kernels  65 us (99%)
    pallas_call x1, Pallas kernels, shards(): pl.pallas_call(kernel, out_shape=(jax.ShapeDtypeStruct((LOCAL, 2, D), BF1...  62.8 us
    pallas_call x1, Pallas kernels, shards(): pl.pallas_call(finish, out_shape=tuple((jax.ShapeDtypeStruct(o.shape, o.d...  2.21 us

profile of v4, /device:TPU:1, one launch (start us, length us, event | category | flops | bytes accessed | tf_op | source)
XLA Modules:
  0.0 65.6 jit_solution(13107268689295575705)
XLA Ops:
  0.6 62.8 %shard_map.102 = (bf16[2,2,1536]{2,1,0:T(2,128)(2,1)}, bf16[2,64,1536]{2,1,0:T(8,128)(2,1)}, bf16[2,128,1536]{2,1,0:T(8,128)(2,1)}, f32[3,1536]{1,0:T(4,128)}) custom-call(bf16[16,64,192]{2,1,0:T(8,128)(2,1)} %att.1, bf16[2,128,1536]{2,1,0:T(8,128)(2,1)} %skip.1, f32[3,1536]{1,0:T(4,128)} %filt_h.1, bf16[192,1536]{1,0:T(8,128)(2,1)} %weight.1, s32[2]{0:T(128)} %offset_h.1, ...), custom_call_target="tpu_custom_call" | custom-call | tf_op jit(solution)/shard_map/pallas_call | solution.py:574
  63.4 2.2 %shard_map.103 = (bf16[2,2,1536]{2,1,0:T(2,128)(2,1)}, bf16[2,64,1536]{2,1,0:T(8,128)(2,1)}, bf16[2,128,1536]{2,1,0:T(8,128)(2,1)}, f32[3,1536]{1,0:T(4,128)}) custom-call(bf16[2,2,1536]{2,1,0:T(2,128)(2,1)} %get-tuple-element.8.a, bf16[2,64,1536]{2,1,0:T(8,128)(2,1)} %get-tuple-element.9.b, bf16[2,128,1536]{2,1,0:T(8,128)(2,1)} %get-tuple-element.10.c, ...), custom_call_target="tpu_custom_call" | custom-call | tf_op jit(solution)/shard_map/pallas_call | solution.py:641

commit v5 on v4

--- a/solution.py
+++ b/solution.py
@@ -29,7 +29,7 @@
 ZL = 2
 COT = 0
 ATT = 2
-Z_SIDES = ((1, -1), (-1, 1), (1, -1), (-1, -1), (1, -1), (-1, 1), (1, -1), (-1, -1))
+Z_SIDES = ((1, -1), (-1, 1), (1, -1), (-1, -1), (1, 1), (-1, -1))
 SCALE = 1.0 / math.sqrt(131072.0)
 
 
@@ -229,6 +229,12 @@
         ref = piece(1 - xl if other else xl, d, zp, *part)
         wz.append((send(ref, ref, wz_ss, wz_rs, k, z_peer(side)), other, d, part))
 
+    own_second = weight.at[pl.ds(pl.multiple_of(c * (KD // 2) + (1 - zp) * quarter, 16), quarter)]
+
+    def second_y():
+        for k, d in ((3, 1), (4, 3)):
+            wy[k] = send(own_second, piece(xl, 0, 1 - zp), wy_ss, wy_rs, k, y_peer(-d))
+
     def to_y(k, other, d):
         dst = piece(1 - xl if other else xl, 0, zp)
         wy[k] = send(dst if other else own, dst, wy_ss, wy_rs, k, y_peer(-d))
@@ -245,8 +251,12 @@
     wy[0].wait_send()
     wy[1].wait_send()
     to_y(2, False, 2)
-    if ATT == 2:
+    if ATT == 3:
+        second_y()
+    if ATT == 2 or ATT == 3:
         start_att()
+    if ATT != 3:
+        second_y()
     if COT == 1:
         cot_copy.start()
 
@@ -256,7 +266,8 @@
 
     def from_y(k, d):
         wy[k].wait_recv()
-        to_z(False, d)
+        if d == 2:
+            to_z(False, d)
         to_core(piece(xl, d, zp))
 
     def from_x(k):
@@ -431,13 +442,16 @@
             core_copies[k].wait_recv()
 
     yh = y // 2
-    from_z(0, 1, 2, 3)
+    for k, d in ((3, 1), (4, 3)):
+        wy[k].wait_recv()
+        to_core(piece(xl, d, 1 - zp))
+    from_z(0, 1)
     from_core(0, 1, 8, 9)
     block(2 * xl + yh)
-    from_z(4, 5)
+    from_z(2, 3)
     from_core(3, 11)
     block(2 * xl + 1 - yh)
-    from_z(6, 7)
+    from_z(4, 5)
     from_core(2, 4, 5, 10, 12, 13)
     block(2 * (1 - xl) + yh)
     from_core(6, 7, 14, 15)

time: 65.8 us -> 63.9 us (0.971)
  Pallas kernels: 65 us -> 63.1 us
    pallas_call x1, Pallas kernels: 62.8 us -> 60.9 us  [shards(): pl.pallas_call(kernel, out_shape=(jax.ShapeDtypeStruct((LOCAL, 2, D), BF1...]
where the time goes in v5:
time: 63.9 us; the launch traced here: 63.8 us
  Pallas kernels  63.1 us (99%)
  between operations  0.64 us (1%)
    pallas_call x1, Pallas kernels, shards(): pl.pallas_call(kernel, out_shape=(jax.ShapeDtypeStruct((LOCAL, 2, D), BF1...  60.9 us
    pallas_call x1, Pallas kernels, shards(): pl.pallas_call(finish, out_shape=tuple((jax.ShapeDtypeStruct(o.shape, o.d...  2.21 us

profile of v5, /device:TPU:1, one launch (start us, length us, event | category | flops | bytes accessed | tf_op | source)
XLA Modules:
  0.0 63.8 jit_solution(12919672896421544721)
XLA Ops:
  0.6 60.9 %shard_map.102 = (bf16[2,2,1536]{2,1,0:T(2,128)(2,1)}, bf16[2,64,1536]{2,1,0:T(8,128)(2,1)}, bf16[2,128,1536]{2,1,0:T(8,128)(2,1)}, f32[3,1536]{1,0:T(4,128)}) custom-call(bf16[16,64,192]{2,1,0:T(8,128)(2,1)} %att.1, bf16[2,128,1536]{2,1,0:T(8,128)(2,1)} %skip.1, f32[3,1536]{1,0:T(4,128)} %filt_h.1, bf16[192,1536]{1,0:T(8,128)(2,1)} %weight.1, s32[2]{0:T(128)} %offset_h.1, ...), custom_call_target="tpu_custom_call" | custom-call | tf_op jit(solution)/shard_map/pallas_call | solution.py:588
  61.5 2.2 %shard_map.103 = (bf16[2,2,1536]{2,1,0:T(2,128)(2,1)}, bf16[2,64,1536]{2,1,0:T(8,128)(2,1)}, bf16[2,128,1536]{2,1,0:T(8,128)(2,1)}, f32[3,1536]{1,0:T(4,128)}) custom-call(bf16[2,2,1536]{2,1,0:T(2,128)(2,1)} %get-tuple-element.8.a, bf16[2,64,1536]{2,1,0:T(8,128)(2,1)} %get-tuple-element.9.b, bf16[2,128,1536]{2,1,0:T(8,128)(2,1)} %get-tuple-element.10.c, ...), custom_call_target="tpu_custom_call" | custom-call | tf_op jit(solution)/shard_map/pallas_call | solution.py:655

commit v6 on v5

--- a/solution.py
+++ b/solution.py
@@ -192,7 +192,7 @@
             cp.start()
             att_copies.append(cp)
 
-    cot_copy = remote(cot, cotbuf.at[:, pl.ds(0, ROWS)], cot_sem.at[0], cot_sem.at[1], next_dev)
+    cot_copy = remote(cotbuf.at[:, pl.ds(ROWS, ROWS)], cotbuf.at[:, pl.ds(0, ROWS)], cot_sem.at[0], cot_sem.at[1], next_dev)
 
     quarter = KD // 4
 
@@ -200,7 +200,9 @@
         row = (xl_ * 4 + (y + d) % 4) * KD + c * (KD // 2) + p * quarter + lo
         return wbuf.at[pl.ds(pl.multiple_of(row, 16), n)]
 
-    own = weight.at[pl.ds(pl.multiple_of(c * (KD // 2) + zp * quarter, 16), quarter)]
+    own_w.wait()
+    own_cot.wait()
+    own = piece(xl, 0, zp)
     wy, wx, wz, core_copies, sent = {}, {}, [], [], []
 
     def send(src, dst, ss, rs, k, dev):
@@ -229,7 +231,7 @@
         ref = piece(1 - xl if other else xl, d, zp, *part)
         wz.append((send(ref, ref, wz_ss, wz_rs, k, z_peer(side)), other, d, part))
 
-    own_second = weight.at[pl.ds(pl.multiple_of(c * (KD // 2) + (1 - zp) * quarter, 16), quarter)]
+    own_second = piece(xl, 0, 1 - zp)
 
     def second_y():
         for k, d in ((3, 1), (4, 3)):
@@ -313,6 +315,7 @@
         cp.wait()
     own_skip.wait()
     stage1()
+    stage2()
     pl.semaphore_wait(z_in.at[1], 2)
     for by in (4, -4):
         greet(z_in.at[2], z_peer(by))
@@ -341,7 +344,6 @@
     for cp in edges:
         cp.start()
 
-    stage2()
     def forward(b, low, n, part=0, parts=1):
         @pl.loop(part * D // TILE // parts, (part + 1) * D // TILE // parts)
         def _(t):
@@ -372,9 +374,7 @@
     for b in range(LOCAL):
         forward(b, 0, 16)
         forward(b, ROWS - 16, 16)
-    own_w.wait()
-
-    own_cot.wait()
+
     cot_copy.wait()
     place = lax.broadcasted_iota(jnp.int32, (ROWS, 2 * ROWS), 1)
     row = lax.broadcasted_iota(jnp.int32, (ROWS, 2 * ROWS), 0)
@@ -471,6 +471,10 @@
     rows_s[...] = block_rows[0:8]
     rows_copy = remote(rows_s.at[pl.ds(4, 4)], rows_r, rows_sem.at[0], rows_sem.at[1], prev_dev)
 
+    far_first = sorted(
+        [(dx, dy, dc) for dx in range(4) for dy in range(4) for dc in range(2) if dx or dy or dc],
+        key=lambda o: -(min(o[0], 4 - o[0]) + min(o[1], 4 - o[1])),
+    )
     t_mine = my_plane % 16
     owns = (t_mine < OWNERS) & (my_plane // 16 == t_mine % 2)
 
@@ -483,7 +487,7 @@
             total = total + plane_r[i]
         zsum[...] = total
         z_r[z] = total
-        for i in range(1, ZS):
+        for i in sorted(range(1, ZS), key=lambda i: -min(i, ZS - i)):
             remote(zsum, z_r.at[z], red_ss.at[1], red_rs.at[1], z_peer(i)).start()
 
     rows_copy.start()
@@ -522,6 +526,23 @@
         whole = rows_s[pl.ds(2 * b, 2), :] + rows_r[pl.ds(2 * b, 2), :] * last
         tgt_out[b] = whole.astype(BF16)
 
+    for cp in out_copies:
+        cp.wait()
+    for cp in att_copies + [q for q in sent if q is not wy[0] and q is not wy[1]] + edges:
+        cp.wait_send()
+
+    @pl.when(owns)
+    def _():
+        part = plane_r.at[pl.ds(0, OWNERS - 1)]
+        pltpu.make_async_copy(part, part, red_ss.at[0]).wait()
+        part = z_r.at[pl.ds(0, ZS - 1)]
+        pltpu.make_async_copy(part, part, red_ss.at[1]).wait()
+
+    @pl.when(jnp.logical_not(owns))
+    def _():
+        part = plane_r.at[pl.ds(0, OWNERS)]
+        pltpu.make_async_copy(part, part, red_ss.at[0]).wait()
+
     @pl.when(owns)
     def _():
         part = z_r.at[pl.ds(0, ZS - 1)]
@@ -532,10 +553,10 @@
         final[...] = total * SCALE
         fin_r[t_mine] = total * SCALE
 
-        for i in range(1, PLANE):
-            remote(
-                final, fin_r.at[t_mine], red_ss.at[2], red_rs.at[2], plane_dev((my_plane + i) % PLANE)
-            ).start()
+        for dx, dy, dc in far_first:
+            other = (x + dx) % 4
+            to = at(z, other // 2, 1 - c if dc else c, other % 2, (y + dy) % 4)
+            remote(final, fin_r.at[t_mine], red_ss.at[2], red_rs.at[2], to).start()
 
     @pl.when(owns)
     def _():
@@ -549,28 +570,16 @@
     for t in range(OWNERS):
         filt_out[:, pl.ds(t * TILE, TILE)] = fin_r[t, pl.ds(0, 3), :]
 
-    for cp in out_copies:
-        cp.wait()
-    for cp in att_copies + [q for q in sent if q is not wy[0] and q is not wy[1]] + edges:
-        cp.wait_send()
-
     @pl.when(owns)
     def _():
-        part = plane_r.at[pl.ds(0, OWNERS - 1)]
-        pltpu.make_async_copy(part, part, red_ss.at[0]).wait()
-        part = z_r.at[pl.ds(0, ZS - 1)]
-        pltpu.make_async_copy(part, part, red_ss.at[1]).wait()
         part = plane_r.at[pl.ds(0, PLANE - 1)]
         pltpu.make_async_copy(part, part, red_ss.at[2]).wait()
 
-    @pl.when(jnp.logical_not(owns))
-    def _():
-        part = plane_r.at[pl.ds(0, OWNERS)]
-        pltpu.make_async_copy(part, part, red_ss.at[0]).wait()
-
 
 def finish(a, b, c, d, a_out, b_out, c_out, d_out, av, bv, cv, dv, sem_in, sem_out):
-    parts = ((c, cv, c_out), (b, bv, b_out), (d, dv, d_out), (a, av, a_out))
+    parts = [(c.at[i], cv.at[i], c_out.at[i]) for i in range(LOCAL)]
+    parts += [(b.at[i], bv.at[i], b_out.at[i]) for i in range(LOCAL)]
+    parts += [(d, dv, d_out), (a, av, a_out)]
     ins = [pltpu.make_async_copy(x, v, sem_in.at[i]) for i, (x, v, _) in enumerate(parts)]
     outs = [pltpu.make_async_copy(v, o, sem_out.at[i]) for i, (_, v, o) in enumerate(parts)]
     for cp in ins:
@@ -657,7 +666,7 @@
         out_shape=tuple(jax.ShapeDtypeStruct(o.shape, o.dtype) for o in outs),
         in_specs=[HBM] * 4,
         out_specs=(HBM,) * 4,
-        scratch_shapes=[pltpu.VMEM(o.shape, o.dtype) for o in outs] + [dma((4,)), dma((4,))],
+        scratch_shapes=[pltpu.VMEM(o.shape, o.dtype) for o in outs] + [dma((6,)), dma((6,))],
         compiler_params=pltpu.CompilerParams(vmem_limit_bytes=60 << 20),
     )(*outs)
 

time: 63.9 us -> 63.5 us (level)
  no operation moved by 1% of the time
where the time goes in v6:
time: 63.5 us; the launch traced here: 63.4 us
  Pallas kernels  62.7 us (99%)
  between operations  0.64 us (1%)
    pallas_call x1, Pallas kernels, shards(): pl.pallas_call(kernel, out_shape=(jax.ShapeDtypeStruct((LOCAL, 2, D), BF1...  60.6 us
    pallas_call x1, Pallas kernels, shards(): pl.pallas_call(finish, out_shape=tuple((jax.ShapeDtypeStruct(o.shape, o.d...  2.11 us

profile of v6, /device:TPU:1, one launch (start us, length us, event | category | flops | bytes accessed | tf_op | source)
XLA Modules:
  0.0 63.4 jit_solution(14876876447112517339)
XLA Ops:
  0.6 60.6 %shard_map.102 = (bf16[2,2,1536]{2,1,0:T(2,128)(2,1)}, bf16[2,64,1536]{2,1,0:T(8,128)(2,1)}, bf16[2,128,1536]{2,1,0:T(8,128)(2,1)}, f32[3,1536]{1,0:T(4,128)}) custom-call(bf16[16,64,192]{2,1,0:T(8,128)(2,1)} %att.1, bf16[2,128,1536]{2,1,0:T(8,128)(2,1)} %skip.1, f32[3,1536]{1,0:T(4,128)} %filt_h.1, bf16[192,1536]{1,0:T(8,128)(2,1)} %weight.1, s32[2]{0:T(128)} %offset_h.1, ...), custom_call_target="tpu_custom_call" | custom-call | tf_op jit(solution)/shard_map/pallas_call | solution.py:597
  61.3 2.1 %shard_map.103 = (bf16[2,2,1536]{2,1,0:T(2,128)(2,1)}, bf16[2,64,1536]{2,1,0:T(8,128)(2,1)}, bf16[2,128,1536]{2,1,0:T(8,128)(2,1)}, f32[3,1536]{1,0:T(4,128)}) custom-call(bf16[2,2,1536]{2,1,0:T(2,128)(2,1)} %get-tuple-element.8.a, bf16[2,64,1536]{2,1,0:T(8,128)(2,1)} %get-tuple-element.9.b, bf16[2,128,1536]{2,1,0:T(8,128)(2,1)} %get-tuple-element.10.c, ...), custom_call_target="tpu_custom_call" | custom-call | tf_op jit(solution)/shard_map/pallas_call | solution.py:664

commit v7 on v6

--- a/solution.py
+++ b/solution.py
@@ -250,8 +250,6 @@
         cot_copy.start()
     if ATT == 1:
         start_att()
-    wy[0].wait_send()
-    wy[1].wait_send()
     to_y(2, False, 2)
     if ATT == 3:
         second_y()
@@ -528,7 +526,7 @@
 
     for cp in out_copies:
         cp.wait()
-    for cp in att_copies + [q for q in sent if q is not wy[0] and q is not wy[1]] + edges:
+    for cp in att_copies + sent + edges:
         cp.wait_send()
 
     @pl.when(owns)

time: 63.5 us -> 63.7 us (level)
  no operation moved by 1% of the time
where the time goes in v7:
time: 63.7 us; the launch traced here: 63.5 us
  Pallas kernels  62.9 us (99%)
  between operations  0.64 us (1%)
    pallas_call x1, Pallas kernels, shards(): pl.pallas_call(kernel, out_shape=(jax.ShapeDtypeStruct((LOCAL, 2, D), BF1...  60.8 us
    pallas_call x1, Pallas kernels, shards(): pl.pallas_call(finish, out_shape=tuple((jax.ShapeDtypeStruct(o.shape, o.d...  2.11 us

profile of v7, /device:TPU:1, one launch (start us, length us, event | category | flops | bytes accessed | tf_op | source)
XLA Modules:
  0.0 63.5 jit_solution(13274827701421778541)
XLA Ops:
  0.6 60.8 %shard_map.102 = (bf16[2,2,1536]{2,1,0:T(2,128)(2,1)}, bf16[2,64,1536]{2,1,0:T(8,128)(2,1)}, bf16[2,128,1536]{2,1,0:T(8,128)(2,1)}, f32[3,1536]{1,0:T(4,128)}) custom-call(bf16[16,64,192]{2,1,0:T(8,128)(2,1)} %att.1, bf16[2,128,1536]{2,1,0:T(8,128)(2,1)} %skip.1, f32[3,1536]{1,0:T(4,128)} %filt_h.1, bf16[192,1536]{1,0:T(8,128)(2,1)} %weight.1, s32[2]{0:T(128)} %offset_h.1, ...), custom_call_target="tpu_custom_call" | custom-call | tf_op jit(solution)/shard_map/pallas_call | solution.py:595
  61.4 2.1 %shard_map.103 = (bf16[2,2,1536]{2,1,0:T(2,128)(2,1)}, bf16[2,64,1536]{2,1,0:T(8,128)(2,1)}, bf16[2,128,1536]{2,1,0:T(8,128)(2,1)}, f32[3,1536]{1,0:T(4,128)}) custom-call(bf16[2,2,1536]{2,1,0:T(2,128)(2,1)} %get-tuple-element.8.a, bf16[2,64,1536]{2,1,0:T(8,128)(2,1)} %get-tuple-element.9.b, bf16[2,128,1536]{2,1,0:T(8,128)(2,1)} %get-tuple-element.10.c, ...), custom_call_target="tpu_custom_call" | custom-call | tf_op jit(solution)/shard_map/pallas_call | solution.py:662
